TPU v7x, 32 devices: a whole 2x2x4 slice. The times are simulated.
32 devices in a mesh: wide: 8 (over z, x), eight: 4 (over y, core).
Axes of the slice: x: 2, y: 2, z: 4, core: 2. Of those that a mesh axis runs over, the one named last changes fastest.
Arguments:
- start_vectors: bfloat16 [128, 96, 4096], P('wide', 'eight'), may hold values from -6 to 6
- conductance: float32 [128, 4096], P('wide'), may hold values from 1 to 100
- counts: int32 [128], P('wide'), may hold values from 1 to 96, as said below
- element_of: int32 [128, 8], P('wide'), may hold values from 0 to 127, as said below
- capacity: float32 [128, 512], P(('wide', 'eight')), may hold values from 0.25 to 4
- coarse_in: float32 [128, 96, 64], P(('wide', 'eight')), may hold values from -6 to 6
Outputs:
- galerkin: float32 [128, 768, 768], P(('wide', 'eight'))
- coarse_out: float32 [128, 96, 64], P(('wide', 'eight'))
Inputs may be any that keep to these rules, and one draw needn't show every extreme that they name: `counts`: some neighbourhood keeps exactly 96 basis functions. For each octant o, element_of[:, o] names every element exactly once. Element e belongs to device e // 4 in the order of wide+eight, and the 16 neighbourhoods of each index of wide name, over all their octants, exactly 4 elements of each device.
All inputs are finite; a program needn't handle non-finite values.
Results may differ from a plain program's by a relative error of at most 0.0004.
Values sent between devices are 32-bit elements; how exact they have to be, the bound alone decides.
No kernel may reach another device: no remote copies, remote signals or barrier semaphores. Data moves between devices by JAX's collectives and lax.ppermute only.
A program may use at most 192 MiB of HBM per device.

v0:
```python
import jax
import jax.numpy as jnp
from jax import lax
from jax.sharding import PartitionSpec as P

SIDE = 16
PASSES = 6
ECELLS = 512


def stencil_weights(conductance, edge_cells):
    cubic_cells = conductance.reshape(conductance.shape[:-1] + (edge_cells, edge_cells, edge_cells))
    leading = cubic_cells.ndim - 3
    padded = jnp.pad(cubic_cells, [(0, 0)] * leading + [(1, 1)] * 3, mode="edge")
    diagonal = jnp.zeros_like(cubic_cells)
    neighbour_links = []
    strides = (edge_cells * edge_cells, edge_cells, 1)
    for direction in range(3):
        position = lax.broadcasted_iota(jnp.int32, cubic_cells.shape, leading + direction)
        for toward in (-1, 1):
            starts = [0] * leading + [1, 1, 1]
            starts[leading + direction] = 1 + toward
            limits = [
                starts[dim_index] + cubic_cells.shape[dim_index]
                for dim_index in range(cubic_cells.ndim)
            ]
            beside = lax.slice(padded, starts, limits)
            face_weight = 0.5 * (cubic_cells + beside)
            diagonal = diagonal + face_weight
            inside = (position + toward >= 0) & (position + toward < edge_cells)
            linked = jnp.where(inside, face_weight, jnp.zeros_like(face_weight))
            neighbour_links.append((toward * strides[direction], linked.reshape(conductance.shape)))
    return (diagonal.reshape(conductance.shape), neighbour_links)


def operate(field, diagonal, neighbour_links, plane_span):
    cell_total = field.shape[-1]
    padded = jnp.pad(field, [(0, 0)] * (field.ndim - 1) + [(plane_span, plane_span)])
    result = diagonal * field
    for offset, linked in neighbour_links:
        moved = lax.slice_in_dim(
            padded, plane_span + offset, plane_span + offset + cell_total, axis=field.ndim - 1
        )
        result = result - linked * moved
    return result


def hat_bump(edge_cells):
    half_side = edge_cells // 2
    along = (jnp.arange(edge_cells, dtype=jnp.float32) + 0.5) / half_side
    rising = jnp.minimum(along, 2.0 - along)
    return (rising[:, None, None] * rising[None, :, None] * rising[None, None, :]).reshape(-1)


def filtered_basis(start, conductance, live, edge_cells, sweeps):
    diagonal, neighbour_links = stencil_weights(conductance, edge_cells)
    upper_bound = 2.0 * jnp.max(diagonal, axis=-1)
    centre = (0.5625 * upper_bound)[..., None, None]
    radius = (0.4375 * upper_bound)[..., None, None]
    diagonal = diagonal[..., None, :]
    neighbour_links = [(offset, linked[..., None, :]) for offset, linked in neighbour_links]
    plane_span = edge_cells * edge_cells
    previous = start
    current = (
        operate(previous, diagonal, neighbour_links, plane_span) - centre * previous
    ) / radius
    for repeat in range(sweeps - 1):
        previous, current = (
            current,
            2.0
            * (operate(current, diagonal, neighbour_links, plane_span) - centre * current)
            / radius
            - previous,
        )
    norm_scale = lax.rsqrt(jnp.mean(current * current, axis=-1, keepdims=True) + 1e-05)
    return current * norm_scale * hat_bump(edge_cells) * live[..., None]


def octant_pieces(basis, edge_cells):
    half_side = edge_cells // 2
    leading = basis.shape[:-1]
    rank_lead = len(leading)
    cubic = basis.reshape(leading + (2, half_side, 2, half_side, 2, half_side))
    axes_order = tuple(range(rank_lead - 1)) + (
        rank_lead,
        rank_lead + 2,
        rank_lead + 4,
        rank_lead - 1,
        rank_lead + 1,
        rank_lead + 3,
        rank_lead + 5,
    )
    cubic = jnp.transpose(cubic, axes_order)
    return cubic.reshape(leading[:-1] + (8, leading[-1], half_side * half_side * half_side))


def body(start_vectors, conductance, counts, element_of, capacity, coarse_in):
    groups = lax.axis_size("eight")
    wide_count = lax.axis_size("wide")
    devices = wide_count * groups
    local_hoods, group_width, cell_total = start_vectors.shape
    per_device = local_hoods // groups
    piece_total = local_hoods * 8
    per_pair = piece_total // devices
    vectors = coarse_in.shape[2]
    slot_ids = lax.axis_index("eight") * group_width + jnp.arange(group_width, dtype=jnp.int32)
    live = (slot_ids[None, :] < counts[:, None]).astype(jnp.float32)
    basis = filtered_basis(start_vectors.astype(jnp.float32), conductance, live, SIDE, PASSES)
    pieces = octant_pieces(basis, SIDE).reshape(piece_total, group_width, ECELLS)
    owner_dev = (element_of // per_device).reshape(-1)
    local_ids = (element_of % per_device * 8 + jnp.arange(8, dtype=jnp.int32)[None, :]).reshape(-1)
    order_ids = jnp.arange(piece_total, dtype=jnp.int32)
    earlier = (owner_dev[:, None] == owner_dev[None, :]) & (order_ids[None, :] < order_ids[:, None])
    target = owner_dev * per_pair + jnp.sum(earlier.astype(jnp.int32), axis=1)
    source_of = jnp.zeros(piece_total, jnp.int32).at[target].set(order_ids)
    coarse_rows = lax.all_to_all(coarse_in, "eight", split_axis=1, concat_axis=0, tiled=True)
    basis_out = pieces[source_of].reshape(devices, per_pair, group_width, ECELLS)
    rows_out = coarse_rows[source_of // 8].reshape(devices, per_pair, group_width, vectors)
    ids_out = local_ids[source_of].reshape(devices, per_pair)
    got_basis, got_rows, got_ids = (
        lax.all_to_all(basis_out, ("wide", "eight"), split_axis=0, concat_axis=0, tiled=True),
        lax.all_to_all(rows_out, ("wide", "eight"), split_axis=0, concat_axis=0, tiled=True),
        lax.all_to_all(ids_out, ("wide", "eight"), split_axis=0, concat_axis=0, tiled=True),
    )
    from_group = (jnp.arange(devices, dtype=jnp.int32) % groups)[:, None]
    position = (got_ids * groups + from_group).reshape(-1)
    slot_of = jnp.zeros(piece_total, jnp.int32).at[position].set(order_ids)
    basis_full = got_basis.reshape(piece_total, group_width, ECELLS)[slot_of].reshape(
        per_device, 8 * groups * group_width, ECELLS
    )
    rows_full = got_rows.reshape(piece_total, group_width, vectors)[slot_of].reshape(
        per_device, 8 * groups * group_width, vectors
    )
    weighted = basis_full * capacity[:, None, :]
    galerkin = (
        jnp.einsum("erc,esc->ers", weighted, basis_full, precision=lax.Precision.HIGHEST) / ECELLS
    )
    applied = jnp.einsum("ers,esv->erv", galerkin, rows_full, precision=lax.Precision.HIGHEST)
    back_out = applied.reshape(piece_total, group_width, vectors)[position].reshape(
        devices, per_pair, group_width, vectors
    )
    returned = lax.all_to_all(back_out, ("wide", "eight"), split_axis=0, concat_axis=0, tiled=True)
    per_piece = returned.reshape(piece_total, group_width, vectors)[target].reshape(
        local_hoods, 8, group_width, vectors
    )
    summed = jnp.sum(per_piece, axis=1)
    coarse_out = lax.all_to_all(summed, "eight", split_axis=0, concat_axis=1, tiled=True)
    return (galerkin, coarse_out)


def solution(mesh):
    in_specs = (
        P("wide", "eight", None),
        P("wide", None),
        P("wide"),
        P("wide", None),
        P(("wide", "eight"), None),
        P(("wide", "eight"), None, None),
    )
    out_specs = (P(("wide", "eight"), None, None), P(("wide", "eight"), None, None))
    return jax.shard_map(body, mesh=mesh, in_specs=in_specs, out_specs=out_specs, check_vma=False)
```

profile of v0, /device:TPU:0, one launch (start us, length us, event | category | flops | bytes accessed | tf_op | source)
XLA Modules:
  0.0 493.6 jit_solution(5640877580559918610)
XLA Ops:
  2.5 4.3 all-to-all-start.2
  10.6 5.6 %fusion.125 = (f32[16]{0:T(128)S(1)}, f32[16,16,16,16]{3,2,1,0:T(8,128)}) fusion(f32[16,16,16,16]{3,2,1,0:T(8,128)S(1)} %reshape.244, f32[16,18,18,1]{3,2,1,0:T(8,128)S(1)} %get-tuple-element.19, f32[16,18,1,16]{3,2,1,0:T(1,128)S(1)} %get-tuple-element.24, f32[16,1,16,16]{3,2,1,0:T(8,128)S(1)} %get-tuple-element.29, ...), kind=kLoop, calls=%fused_computation.234 | loop fusion | flops 2359280 | bytes 635456 | tf_op jit(solution)/shard_map/reduce_max | solution.py:57
  16.2 5.1 %broadcast_select_fusion.1 = (f32[16,16,16,16]{3,2,1,0:T(8,128)}, f32[16,16,16,16]{3,2,1,0:T(8,128)}, f32[16,16,16,16]{3,2,1,0:T(8,128)}) fusion(pred[16]{0:T(512)(128)(4,1)S(1)} %get-tuple-element.36, f32[16,16,16,16]{3,2,1,0:T(8,128)S(1)} %reshape.244, f32[16,18,1,16]{3,2,1,0:T(1,128)S(1)} %get-tuple-element.24, ...), kind=kLoop, calls=%fused_computation.181 | loop fusion | flops 1441792 | bytes 1159712 | tf_op jit(solution)/shard_map/jit(_where)/select_n | solution.py:31
  21.3 3.9 fusion.111
  52.6 7.7 %fusion.10 = f32[16,24,4096]{2,1,0:T(8,128)S(1)} fusion(f32[16,24,4096]{2,1,0:T(8,128)S(1)} %convert_element_type.20, f32[16]{0:T(128)S(1)} %get-tuple-element.34, f32[16]{0:T(128)S(1)} %get-tuple-element.33, f32[16,4096]{1,0:T(8,128)S(1)} %mul.509, f32[16,4096]{1,0:T(8,128)S(1)} %mul.506, f32[16,4096]{1,0:T(8,128)S(1)} %mul.503, f32[16,4096]{1,0:T(8,128)S(1)} %mul.500, ...), kind=kLoop, calls=%fused_computation.55 | loop fusion | flops 25165824 | bytes 14418048 | tf_op jit(solution)/shard_map/div | solution.py:64
  60.3 8.7 %fusion.26 = f32[16,24,4096]{2,1,0:T(8,128)} fusion(f32[16,24,4096]{2,1,0:T(8,128)S(1)} %fusion.10, f32[16]{0:T(128)S(1)} %get-tuple-element.34, f32[16]{0:T(128)S(1)} %get-tuple-element.33, f32[16,4096]{1,0:T(8,128)S(1)} %mul.509, f32[16,4096]{1,0:T(8,128)S(1)} %mul.506, f32[16,4096]{1,0:T(8,128)S(1)} %mul.503, f32[16,4096]{1,0:T(8,128)S(1)} %mul.500, ...), kind=kLoop, calls=%fused_computation.71 | loop fusion | flops 29884416 | bytes 17563776 | tf_op jit(solution)/shard_map/sub | solution.py:70
  69.1 45.9 %fusion.42 = f32[16,24,4096]{2,1,0:T(8,128)} fusion(f32[16,24,4096]{2,1,0:T(8,128)} %fusion.26, f32[16]{0:T(128)S(1)} %get-tuple-element.34, f32[16]{0:T(128)S(1)} %get-tuple-element.33, f32[16,4096]{1,0:T(8,128)S(1)} %mul.509, f32[16,4096]{1,0:T(8,128)S(1)} %mul.506, f32[16,4096]{1,0:T(8,128)S(1)} %mul.503, f32[16,4096]{1,0:T(8,128)S(1)} %mul.500, ...), kind=kLoop, calls=%fused_computation.87 | loop fusion | flops 53477376 | bytes 20709504 | tf_op jit(solution)/shard_map/sub | solution.py:70
  115.0 25.3 %fusion.58 = f32[16,24,4096]{2,1,0:T(8,128)S(1)} fusion(f32[16,24,4096]{2,1,0:T(8,128)} %fusion.26, f32[16,24,4096]{2,1,0:T(8,128)} %fusion.42, f32[16]{0:T(128)S(1)} %get-tuple-element.34, f32[16]{0:T(128)S(1)} %get-tuple-element.33, f32[16,4096]{1,0:T(8,128)S(1)} %mul.509, f32[16,4096]{1,0:T(8,128)S(1)} %mul.506, f32[16,4096]{1,0:T(8,128)S(1)} %mul.503, ...), kind=kLoop, calls=%fused_computation.103 | loop fusion | flops 28311552 | bytes 20709504 | tf_op jit(solution)/shard_map/sub | solution.py:70
  140.3 7.4 %fusion.74 = f32[16,24,4096]{2,1,0:T(8,128)S(1)} fusion(f32[16,24,4096]{2,1,0:T(8,128)S(1)} %copy-done.2, f32[16,24,4096]{2,1,0:T(8,128)S(1)} %fusion.58, f32[16]{0:T(128)S(1)} %get-tuple-element.34, f32[16]{0:T(128)S(1)} %get-tuple-element.33, f32[16,4096]{1,0:T(8,128)S(1)} %mul.509, f32[16,4096]{1,0:T(8,128)S(1)} %mul.506, f32[16,4096]{1,0:T(8,128)S(1)} %mul.503, ...), kind=kLoop, calls=%fused_computation.119 | loop fusion | flops 28311552 | bytes 20709504 | tf_op jit(solution)/shard_map/sub | solution.py:70
  147.7 9.3 %multiply_reduce_fusion = (f32[16,24]{1,0:T(8,128)S(1)}, f32[16,24,4096]{2,1,0:T(8,128)}) fusion(f32[16,24,4096]{2,1,0:T(8,128)S(1)} %fusion.58, f32[16]{0:T(128)S(1)} %get-tuple-element.34, f32[16,24,4096]{2,1,0:T(8,128)S(1)} %fusion.74, f32[16]{0:T(128)S(1)} %get-tuple-element.33, f32[16,4096]{1,0:T(8,128)S(1)} %mul.509, f32[16,4096]{1,0:T(8,128)S(1)} %mul.506, ...), kind=kLoop, calls=%fused_computation.142 | loop fusion | flops 31456896 | bytes 20711040 | tf_op jit(solution)/shard_map/reduce_sum | solution.py:75
  160.9 6.8 %all-to-all-start.1 = ((s32[32,1,4]{2,1,0:T(1,128)}), s32[32,1,4]{2,1,0:T(1,128)S(1)}, u32[]{:S(2)}, u32[]{:S(2)}) async-start(s32[32,1,4]{2,1,0:T(1,128)} %bitcast.7), calls=%async_computation.1 | async-start | bytes 32768 | tf_op jit(solution)/shard_map/all_to_all | solution.py:123
  178.1 6.9 %multiply_multiply_fusion = f32[16,24,4096]{2,1,0:T(8,128)} fusion(f32[16,24,4096]{2,1,0:T(8,128)} %get-tuple-element.15, f32[16,24]{1,0:T(8,128)S(1)} %compare_convert_fusion, f32[4096]{0:T(1024)S(1)} %mul.572, f32[16,24]{1,0:T(8,128)S(1)} %add_rsqrt_fusion), kind=kLoop, calls=%fused_computation.141 | loop fusion | flops 4718592 | bytes 12602368 | tf_op jit(solution)/shard_map/mul | solution.py:76
  185.0 17.6 %copy.62 = f32[16,24,4096]{1,2,0:T(8,128)} copy(f32[16,24,4096]{2,1,0:T(8,128)} %multiply_multiply_fusion) | data formatting | bytes 12582912 | tf_op jit(solution)/shard_map/mul | solution.py:76
  202.6 23.3 %copy.63 = f32[16,2,2,2,24,8,8,8]{4,7,6,5,3,2,1,0:T(8,128)} copy(f32[16,2,2,2,24,8,8,8]{4,7,3,6,2,5,1,0:T(8,128)} %bitcast.51) | data formatting | bytes 12582912 | tf_op jit(solution)/shard_map/transpose | solution.py:93
  225.9 23.2 %gather_fusion = f32[128,24,512]{1,2,0:T(8,128)} fusion(f32[128,24,512]{1,2,0:T(8,128)} %bitcast.53, s32[1024]{0:T(1024)S(1)} %get-tuple-element.38), kind=kCustom, calls=%fused_computation | custom fusion | bytes 12583424 | tf_op jit(solution)/shard_map/gather | solution.py:117
  249.1 20.4 %copy.66 = f32[32,4,24,512]{3,2,1,0:T(8,128)} copy(f32[32,4,24,512]{2,3,1,0:T(8,128)} %bitcast.54) | data formatting | bytes 12582912 | tf_op jit(solution)/shard_map/reshape | solution.py:117
  269.5 5.9 %all-to-all-start = ((f32[32,4,24,512]{3,2,1,0:T(8,128)}), f32[32,4,24,512]{3,2,1,0:T(8,128)}, u32[]{:S(2)}, u32[]{:S(2)}) async-start(f32[32,4,24,512]{3,2,1,0:T(8,128)} %copy.66), calls=%async_computation | async-start | bytes 12582912 | tf_op jit(solution)/shard_map/all_to_all | solution.py:121
  280.9 134.4 %all-to-all-done = f32[32,4,24,512]{3,2,1,0:T(8,128)} async-done(((f32[32,4,24,512]{3,2,1,0:T(8,128)}), f32[32,4,24,512]{3,2,1,0:T(8,128)}, u32[]{:S(2)}, u32[]{:S(2)}) %all-to-all-start) | async-done | bytes 6291488 | tf_op jit(solution)/shard_map/all_to_all | solution.py:121
  415.4 6.5 %gather_fusion.2 = f32[128,24,512]{2,1,0:T(8,128)} fusion(f32[128,24,512]{2,1,0:T(8,128)} %bitcast.6, s32[1024]{0:T(1024)S(1)} %pad_clamp_fusion.3), kind=kCustom, calls=%fused_computation.2 | custom fusion | bytes 12583424 | tf_op jit(solution)/shard_map/gather | solution.py:128
  421.8 21.5 %broadcast_multiply_fusion = f32[4,768,768]{2,1,0:T(8,128)S(1)} fusion(f32[4,768,512]{2,1,0:T(8,128)} %bitcast.52, f32[4,512]{1,0:T(4,128)S(1)} %copy-done.4), kind=kOutput, calls=%fused_computation.143 | convolution fusion | flops 14499446784 | bytes 15736832 | tf_op jit(solution)/shard_map/erc,esc->ers/dot_general | solution.py:136
  443.3 8.0 %fusion.128 = f32[4,768,64]{2,1,0:T(8,128)S(1)} fusion(f32[4,768,768]{2,1,0:T(8,128)S(1)} %broadcast_multiply_fusion, f32[4,768,64]{2,1,0:T(8,128)S(1)} %bitcast.56), kind=kOutput, calls=%fused_computation.237 | convolution fusion | flops 1811939328 | bytes 11010048 | tf_op jit(solution)/shard_map/ers,esv->erv/dot_general | solution.py:138
  454.0 5.7 %all-to-all-start.4 = ((f32[32,1,6144]{2,1,0:T(1,128)}), f32[32,1,6144]{2,1,0:T(1,128)S(1)}, u32[]{:S(2)}, u32[]{:S(2)}) async-start(f32[32,1,6144]{2,1,0:T(1,128)} %reshape.349), calls=%async_computation.4 | async-start | bytes 1572864 | tf_op jit(solution)/shard_map/all_to_all | solution.py:142
  459.7 20.6 %all-to-all-done.4 = f32[32,1,6144]{2,1,0:T(1,128)S(1)} async-done(((f32[32,1,6144]{2,1,0:T(1,128)}), f32[32,1,6144]{2,1,0:T(1,128)S(1)}, u32[]{:S(2)}, u32[]{:S(2)}) %all-to-all-start.4) | async-done | bytes 786464 | tf_op jit(solution)/shard_map/all_to_all | solution.py:142
  484.5 6.9 %all_to_all.60 = f32[4,1,6144]{2,1,0:T(1,128)S(1)} all-to-all(f32[4,1,6144]{2,1,0:T(1,128)S(1)} %reshape.351), channel_id=1, replica_groups=mesh['wide'=8,'eight'=4] {'eight'}, dimensions={0} | all-to-all | bytes 196608 | tf_op jit(solution)/shard_map/all_to_all | solution.py:147
  (90 shorter events, 61.2 us)
Async XLA Ops:
  2.5 158.4 %all-to-all-start.2 = ((f32[4,1,6144]{2,1,0:T(1,128)}), f32[4,1,6144]{2,1,0:T(1,128)S(1)}, u32[]{:S(2)}, u32[]{:S(2)}) async-start(f32[4,1,6144]{2,1,0:T(1,128)} %reshape.345), calls=%async_computation.2 | async-start | bytes 196608 | tf_op jit(solution)/shard_map/all_to_all | solution.py:116
  49.9 2.7 copy-start.1
  52.6 7.7 %copy-start.3 = (bf16[16,24,4096]{2,1,0:T(8,128)(2,1)S(1)}, bf16[16,24,4096]{2,1,0:T(8,128)(2,1)}, u32[]{:S(2)}) copy-start(bf16[16,24,4096]{2,1,0:T(8,128)(2,1)} %param.6) | copy-start | bytes 9437188
  115.0 25.3 %copy-start.2 = (f32[16,24,4096]{2,1,0:T(8,128)S(1)}, f32[16,24,4096]{2,1,0:T(8,128)}, u32[]{:S(2)}) copy-start(f32[16,24,4096]{2,1,0:T(8,128)} %fusion.42) | copy-start | bytes 18874372
  147.7 9.5 %copy-start.5 = (s32[16,8]{0,1:T(8,128)S(1)}, s32[16,8]{0,1:T(8,128)}, u32[]{:S(2)}) copy-start(s32[16,8]{0,1:T(8,128)} %param.9) | copy-start | bytes 1540
  157.1 20.8 %copy-start.6 = (s32[16]{0:T(128)S(1)}, s32[16]{0:T(128)}, u32[]{:S(2)}) copy-start(s32[16]{0:T(128)} %param.8) | copy-start | bytes 196
  160.9 14.0 %all-to-all-start.1 = ((s32[32,1,4]{2,1,0:T(1,128)}), s32[32,1,4]{2,1,0:T(1,128)S(1)}, u32[]{:S(2)}, u32[]{:S(2)}) async-start(s32[32,1,4]{2,1,0:T(1,128)} %bitcast.7), calls=%async_computation.1 | async-start | bytes 32768 | tf_op jit(solution)/shard_map/all_to_all | solution.py:123
  174.9 94.6 %all-to-all-start.3 = ((f32[32,1,6144]{2,1,0:T(1,128)}), f32[32,1,6144]{2,1,0:T(1,128)S(1)}, u32[]{:S(2)}, u32[]{:S(2)}) async-start(f32[32,1,6144]{2,1,0:T(1,128)} %reshape.347), calls=%async_computation.3 | async-start | bytes 1572864 | tf_op jit(solution)/shard_map/all_to_all | solution.py:122
  269.5 145.8 %all-to-all-start = ((f32[32,4,24,512]{3,2,1,0:T(8,128)}), f32[32,4,24,512]{3,2,1,0:T(8,128)}, u32[]{:S(2)}, u32[]{:S(2)}) async-start(f32[32,4,24,512]{3,2,1,0:T(8,128)} %copy.66), calls=%async_computation | async-start | bytes 12582912 | tf_op jit(solution)/shard_map/all_to_all | solution.py:121
  415.3 6.5 %copy-start.4 = (f32[4,512]{1,0:T(4,128)S(1)}, f32[4,512]{1,0:T(4,128)}, u32[]{:S(2)}) copy-start(f32[4,512]{1,0:T(4,128)} %param.10) | copy-start | bytes 24580
  443.3 8.1 %copy-start = (f32[4,768,768]{2,1,0:T(8,128)}, f32[4,768,768]{2,1,0:T(8,128)S(1)}, u32[]{:S(2)}) copy-start(f32[4,768,768]{2,1,0:T(8,128)S(1)} %broadcast_multiply_fusion) | copy-start | bytes 28311556
  454.0 26.3 %all-to-all-start.4 = ((f32[32,1,6144]{2,1,0:T(1,128)}), f32[32,1,6144]{2,1,0:T(1,128)S(1)}, u32[]{:S(2)}, u32[]{:S(2)}) async-start(f32[32,1,6144]{2,1,0:T(1,128)} %reshape.349), calls=%async_computation.4 | async-start | bytes 1572864 | tf_op jit(solution)/shard_map/all_to_all | solution.py:142
where the time goes:
time: 501 us; the launch traced here: 494 us
  waiting for transfers between devices  158 us (32%)
  other arithmetic  137 us (27%)
  local copies, waits for them, and re-layouts  135 us (27%)
  matrix products  29.5 us (6%)
  starting transfers between devices  25.6 us (5%)
  blocking collectives  6.85 us (1%)
    all_to_all x1, waiting for transfers between devices, body(): lax.all_to_all(basis_out, ('wide', 'eight'), split_axis=0, concat_axis=0,...  134 us
    sub x4, other arithmetic, filtered_basis(): 2.0 * (operate(current, diagonal, neighbour_links, plane_span) - centre *...  87.3 us
    transpose x1, local copies, waits for them, and re-layouts, octant_pieces(): cubic = jnp.transpose(cubic, axes_order)  23.3 us
    gather x1, local copies, waits for them, and re-layouts, body(): pieces[source_of].reshape(devices, per_pair, group_width, ECELLS)  23.2 us
    dot_general x1, matrix products, body(): jnp.einsum('erc,esc->ers', weighted, basis_full, precision=lax.Precision....  21.5 us
    all_to_all x1, waiting for transfers between devices, body(): lax.all_to_all(back_out, ('wide', 'eight'), split_axis=0, concat_axis=0,...  20.6 us
    reshape x1, local copies, waits for them, and re-layouts, body(): pieces[source_of].reshape(devices, per_pair, group_width, ECELLS)  20.4 us
    mul x6, local copies, waits for them, and re-layouts, operate(): result = result - linked * moved  18.9 us
  transfers between devices with their start and end apart: 5, of which 3 were waited for; matrix products, arithmetic and copies ran while one was open for 51% of the time, Pallas kernels for 0%

commit v1 on v0

v1 whole, which is shorter than its diff:
```python
import functools

import jax
import jax.numpy as jnp
from jax import lax
from jax.experimental import pallas as pl
from jax.experimental.pallas import tpu as pltpu
from jax.sharding import PartitionSpec as P

SIDE = 16
PASSES = 6
ECELLS = 512
LANES = 128
ROWS = 8
HALF = SIDE // 2
TILES = SIDE * SIDE * SIDE // LANES
PAIR = SIDE * SIDE // LANES

ANY = pl.BlockSpec(memory_space=pl.ANY)
VMEM = pl.BlockSpec(memory_space=pltpu.VMEM)
SMEM = pl.BlockSpec(memory_space=pltpu.SMEM)


def hat(i):
    return min(i + 0.5, SIDE - 0.5 - i) / HALF


def stencil_table(cond, w_ref):
    cells = cond.shape[1]
    at = lax.broadcasted_iota(jnp.int32, cond.shape, 1)
    diagonal = jnp.zeros_like(cond)
    links = []
    for stride in (SIDE * SIDE, SIDE, 1):
        position = (at // stride) % SIDE
        for toward in (-1, 1):
            beside = pltpu.roll(cond, (-toward * stride) % cells, 1)
            inside = (position + toward >= 0) & (position + toward < SIDE)
            face = 0.5 * (cond + jnp.where(inside, beside, cond))
            diagonal = diagonal + face
            links.append(jnp.where(inside, face, 0.0))
    upper = 2.0 * jnp.max(diagonal, axis=1, keepdims=True)
    twice = 2.0 / (0.4375 * upper)
    table = [(diagonal - 0.5625 * upper) * twice] + [link * twice for link in links]
    for i, values in enumerate(table):
        for t in range(TILES):
            w_ref[i, t] = values[:, t * LANES : (t + 1) * LANES]


def filter_kernel(first_slot, groups, target_ref, counts_ref, sv_ref, cond_ref, send_ref, w_ref, y_ref, out_ref, sems):
    n = pl.program_id(0)
    last = pl.num_programs(0) - 1
    rows = groups * ROWS
    lane = lax.broadcasted_iota(jnp.int32, (ROWS, LANES), 1)
    low_row = lane < SIDE
    high_row = lane >= LANES - SIDE

    @pl.when(n == 0)
    def _():
        stencil_table(cond_ref[...], w_ref)

    def weight(k, t):
        return w_ref[k, t, pl.ds(n, ROWS, 0), :]

    start = sv_ref[0].astype(jnp.float32)
    for g in range(groups):
        y_ref[0, g] = start[first_slot + g * ROWS : first_slot + (g + 1) * ROWS, :]

    squares = [jnp.zeros((ROWS, LANES), jnp.float32) for _ in range(groups)]
    for sweep in range(PASSES):
        src, dst, old = sweep % 3, (sweep + 1) % 3, (sweep + 2) % 3

        def tile(g, a, d):
            t = a * PAIR + d
            return y_ref[src, g, :, t * LANES : (t + 1) * LANES]

        window = [[None] + [[tile(g, a, d) for d in range(PAIR)] for a in range(1)] for g in range(groups)]
        for a in range(SIDE):
            ups = []
            for g in range(groups):
                below, here = window[g]
                above = [tile(g, a + 1, d) for d in range(PAIR)] if a + 1 < SIDE else None
                ups.append((below, here, above))
                window[g] = [here, above]
            back = [[pltpu.roll(u[1][d], SIDE, 1) for d in range(PAIR)] for u in ups]
            fore = [[pltpu.roll(u[1][d], LANES - SIDE, 1) for d in range(PAIR)] for u in ups]
            for d in range(PAIR):
                t = a * PAIR + d
                w = [weight(k, t) for k in range(7)]
                for g in range(groups):
                    below, here, above = ups[g]
                    value = w[0] * here[d]
                    if below is not None:
                        value = value - w[1] * below[d]
                    if above is not None:
                        value = value - w[2] * above[d]
                    lower = back[g][d] if d == 0 else jnp.where(low_row, back[g][d - 1], back[g][d])
                    upper = fore[g][d] if d == PAIR - 1 else jnp.where(high_row, fore[g][d + 1], fore[g][d])
                    value = value - w[3] * lower
                    value = value - w[4] * upper
                    value = value - w[5] * pltpu.roll(here[d], 1, 1)
                    value = value - w[6] * pltpu.roll(here[d], LANES - 1, 1)
                    if sweep == 0:
                        value = 0.5 * value
                    else:
                        value = value - y_ref[old, g, :, t * LANES : (t + 1) * LANES]
                    y_ref[dst, g, :, t * LANES : (t + 1) * LANES] = value
                    if sweep == PASSES - 1:
                        squares[g] = squares[g] + value * value
    final = PASSES % 3

    slot = lax.rem(n, 2)

    def copy_out(step_slot, piece, o):
        return pltpu.make_async_copy(out_ref.at[step_slot, o], send_ref.at[piece], sems.at[step_slot, o])

    @pl.when(n >= 2)
    def _():
        for o in range(8):
            copy_out(slot, 0, o).wait()

    column = lax.rem(lax.div(lane, SIDE), HALF)
    across = (lax.rem(lane, SIDE)).astype(jnp.float32)
    hat_c = jnp.minimum(across + 0.5, SIDE - 0.5 - across) / HALF
    even = lax.rem(lax.div(lane, HALF), 2) == 0
    bumps = []
    for d in range(PAIR):
        along = (column + d * HALF).astype(jnp.float32)
        bumps.append(hat_c * (jnp.minimum(along + 0.5, SIDE - 0.5 - along) / HALF))
    base = lax.axis_index("eight") * sv_ref.shape[1] + first_slot
    for g in range(groups):
        mean = jnp.sum(squares[g], axis=1, keepdims=True) / (TILES * LANES)
        row = lax.broadcasted_iota(jnp.int32, (ROWS, 1), 0) + (base + g * ROWS)
        scale = lax.rsqrt(mean + 1e-05) * (row < counts_ref[n]).astype(jnp.float32)
        for d in range(PAIR):
            weight_d = scale * bumps[d]
            for dx in range(2):
                for p in range(HALF // 2):
                    pair = []
                    for h in range(2):
                        a = dx * HALF + h * (HALF // 2) + p
                        t = a * PAIR + d
                        pair.append(y_ref[final, g, :, t * LANES : (t + 1) * LANES] * (weight_d * hat(a)))
                    near = jnp.where(even, pair[0], pltpu.roll(pair[1], HALF, 1))
                    far = jnp.where(even, pltpu.roll(pair[0], LANES - HALF, 1), pair[1])
                    for dz, value in enumerate((near, far)):
                        out_ref[slot, dx * 4 + d * 2 + dz, g * ROWS : (g + 1) * ROWS, p * LANES : (p + 1) * LANES] = value
    for o in range(8):
        copy_out(slot, target_ref[n * 8 + o], o).start()

    @pl.when(n == last)
    def _():
        for o in range(8):
            copy_out(1 - slot, 0, o).wait()
        for o in range(8):
            copy_out(slot, 0, o).wait()


def filter_call(first_slot, groups, target, counts, start_vectors, conductance):
    hoods, width, cells = start_vectors.shape
    rows = groups * ROWS
    return pl.pallas_call(
        functools.partial(filter_kernel, first_slot, groups),
        grid_spec=pltpu.PrefetchScalarGridSpec(
            num_scalar_prefetch=2,
            grid=(hoods,),
            in_specs=[
                pl.BlockSpec((1, width, cells), lambda n, t, c: (n, 0, 0)),
                pl.BlockSpec((hoods, cells), lambda n, t, c: (0, 0)),
            ],
            out_specs=ANY,
            scratch_shapes=[
                pltpu.VMEM((7, TILES, hoods, LANES), jnp.float32),
                pltpu.VMEM((3, groups, ROWS, cells), jnp.float32),
                pltpu.VMEM((2, 8, rows, ECELLS), jnp.float32),
                pltpu.SemaphoreType.DMA((2, 8)),
            ],
        ),
        out_shape=jax.ShapeDtypeStruct((hoods * 8, rows, ECELLS), jnp.float32),
        name="filter%d" % first_slot,
    )(target, counts, start_vectors, conductance)


def pack(blocks):
    if len(blocks) % 2:
        blocks = blocks + [jnp.zeros_like(blocks[0])]
    return [jnp.concatenate(blocks[i : i + 2], axis=1) for i in range(0, len(blocks), 2)]


def half(tile, k):
    vectors = LANES // 2
    return tile[:, (k % 2) * vectors : (k % 2 + 1) * vectors]


def packed_width(blocks):
    return (blocks + 1) // 2 * LANES


def coarse_pack_kernel(groups, in_ref, out_ref):
    owned, slots, _ = in_ref.shape
    width = slots // groups
    for e in range(groups):
        blocks = [
            in_ref[n, e * width + r : e * width + r + ROWS, :] for n in range(owned) for r in range(0, width, ROWS)
        ]
        for i, tile in enumerate(pack(blocks)):
            out_ref[e, :, i * LANES : (i + 1) * LANES] = tile


def rows_kernel(per_pair, target_ref, in_ref, out_ref, rows_ref, source_ref):
    groups = in_ref.shape[0]
    hoods, width, _ = rows_ref.shape
    owned = hoods // groups
    bits = width // ROWS
    for e in range(groups):
        for n in range(owned):
            for r in range(bits):
                k = n * bits + r
                rows_ref[e * owned + n, r * ROWS : (r + 1) * ROWS, :] = half(
                    in_ref[e, :, k // 2 * LANES : (k // 2 + 1) * LANES], k
                )

    def invert(p, carry):
        source_ref[target_ref[p]] = p
        return carry

    lax.fori_loop(0, hoods * 8, invert, 0)

    def place(d, carry):
        blocks = []
        for i in range(per_pair):
            n = lax.div(source_ref[d * per_pair + i], 8)
            blocks += [rows_ref[n, r * ROWS : (r + 1) * ROWS, :] for r in range(bits)]
        for i, tile in enumerate(pack(blocks)):
            out_ref[d, :, i * LANES : (i + 1) * LANES] = tile
        return carry

    lax.fori_loop(0, out_ref.shape[0], place, 0)


def sum_kernel(per_pair, target_ref, in_ref, out_ref, rows_ref, source_ref):
    groups = out_ref.shape[0]
    hoods, width, _ = rows_ref.shape
    owned = hoods // groups
    bits = width // ROWS
    rows_ref[...] = jnp.zeros_like(rows_ref)

    def invert(p, carry):
        source_ref[target_ref[p]] = p
        return carry

    lax.fori_loop(0, hoods * 8, invert, 0)

    def gather(d, carry):
        for i in range(per_pair):
            n = lax.div(source_ref[d * per_pair + i], 8)
            for r in range(bits):
                k = i * bits + r
                rows_ref[n, r * ROWS : (r + 1) * ROWS, :] += half(in_ref[d, :, k // 2 * LANES : (k // 2 + 1) * LANES], k)
        return carry

    lax.fori_loop(0, in_ref.shape[0], gather, 0)
    for e in range(groups):
        blocks = [
            rows_ref[e * owned + n, r * ROWS : (r + 1) * ROWS, :] for n in range(owned) for r in range(bits)
        ]
        for i, tile in enumerate(pack(blocks)):
            out_ref[e, :, i * LANES : (i + 1) * LANES] = tile


def coarse_out_kernel(in_ref, out_ref):
    groups = in_ref.shape[0]
    owned, slots, _ = out_ref.shape
    width = slots // groups
    bits = width // ROWS
    for e in range(groups):
        for n in range(owned):
            for r in range(bits):
                k = n * bits + r
                out_ref[n, e * width + r * ROWS : e * width + (r + 1) * ROWS, :] = half(
                    in_ref[e, :, k // 2 * LANES : (k // 2 + 1) * LANES], k
                )


def split(x):
    high = x.astype(jnp.bfloat16)
    return high, (x - high.astype(jnp.float32)).astype(jnp.bfloat16)


def product(x, y, dims):
    xh, xl = x
    yh, yl = y
    dot = functools.partial(lax.dot_general, dimension_numbers=(dims, ((), ())), preferred_element_type=jnp.float32)
    return dot(xh, yh) + (dot(xh, yl) + dot(xl, yh))


def gather_basis(chunks, groups, per_pair, ids_ref, got_refs, phi_ref, sems):
    width = sum(count for _, count in chunks) * ROWS
    stride = groups * width
    pieces = ids_ref.shape[0]

    def place(q, carry):
        row = ids_ref[q] * stride + lax.rem(lax.div(q, per_pair), groups) * width
        for k, (first, count) in enumerate(chunks):
            rows = count * ROWS
            pltpu.make_async_copy(
                got_refs[k].at[pl.ds(pl.multiple_of(q * rows, ROWS), rows)],
                phi_ref.at[pl.ds(pl.multiple_of(row + first, ROWS), rows)],
                sems.at[k],
            ).start()
        return carry

    lax.fori_loop(0, pieces, place, 0)
    for k, (first, count) in enumerate(chunks):
        pltpu.make_async_copy(got_refs[k], phi_ref.at[pl.ds(0, pieces * count * ROWS)], sems.at[k]).wait()


def applied_kernel(chunks, groups, per_pair, ids_ref, rows_in_ref, cap_ref, *refs):
    got_refs = refs[: len(chunks)]
    out_ref, phi_ref, r_ref, applied_ref, sems = refs[len(chunks) :]
    width = sum(count for _, count in chunks) * ROWS
    bits = width // ROWS
    stride = groups * width
    elements = cap_ref.shape[0]
    devices = rows_in_ref.shape[0]
    gather_basis(chunks, groups, per_pair, ids_ref, got_refs, phi_ref, sems)

    def row_of(s, i):
        return ids_ref[s * per_pair + i] * stride + lax.rem(s, groups) * width

    def place(s, carry):
        for i in range(per_pair):
            row = row_of(s, i)
            for r in range(bits):
                k = i * bits + r
                r_ref[pl.ds(pl.multiple_of(row + r * ROWS, ROWS), ROWS), :] = half(
                    rows_in_ref[s, :, k // 2 * LANES : (k // 2 + 1) * LANES], k
                )
        return carry

    lax.fori_loop(0, devices, place, 0)
    rows = 8 * stride
    for e in range(elements):
        phi = split(phi_ref[e * rows : (e + 1) * rows, :])
        r = split(jnp.transpose(r_ref[e * rows : (e + 1) * rows, :]))
        sums = product(r, phi, ((1,), (0,))) * cap_ref[e : e + 1, :]
        applied_ref[e * rows : (e + 1) * rows, :] = product(phi, split(sums), ((1,), (1,)))

    def back(s, carry):
        blocks = []
        for i in range(per_pair):
            row = row_of(s, i)
            blocks += [applied_ref[pl.ds(pl.multiple_of(row + r * ROWS, ROWS), ROWS), :] for r in range(bits)]
        for i, tile in enumerate(pack(blocks)):
            out_ref[s, :, i * LANES : (i + 1) * LANES] = tile
        return carry

    lax.fori_loop(0, devices, back, 0)


def galerkin_kernel(chunks, groups, per_pair, ids_ref, cap_ref, *refs):
    got_refs = refs[: len(chunks)]
    out_ref, phi_ref, sems = refs[len(chunks) :]
    width = sum(count for _, count in chunks) * ROWS
    rows = 8 * groups * width
    e = pl.program_id(0)

    @pl.when(e == 0)
    def _():
        gather_basis(chunks, groups, per_pair, ids_ref, got_refs, phi_ref, sems)

    phi = phi_ref[pl.ds(pl.multiple_of(e * rows, ROWS), rows), :]
    weighted = phi * cap_ref[pl.ds(e, 1), :]
    out_ref[0] = product(split(weighted), split(phi), ((1,), (1,)))


CHUNKS = ((0, 1), (8, 2))


def whole(f, shape, *args, scratch=(), prefetch=0, name=None):
    return pl.pallas_call(
        f,
        grid_spec=pltpu.PrefetchScalarGridSpec(
            num_scalar_prefetch=prefetch,
            grid=(),
            in_specs=[VMEM] * (len(args) - prefetch),
            out_specs=VMEM,
            scratch_shapes=list(scratch),
        ),
        out_shape=jax.ShapeDtypeStruct(shape, jnp.float32),
        name=name,
    )(*args)


def body(start_vectors, conductance, counts, element_of, capacity, coarse_in):
    groups = lax.axis_size("eight")
    devices = lax.axis_size("wide") * groups
    hoods, width, cells = start_vectors.shape
    owned = hoods // groups
    elements = capacity.shape[0]
    pieces = hoods * 8
    per_pair = pieces // devices
    slots, vectors = coarse_in.shape[1:]
    bits = width // ROWS
    chunks = CHUNKS
    both = ("wide", "eight")

    owner = (element_of // elements).reshape(-1)
    local = (element_of % elements * 8 + jnp.arange(8, dtype=jnp.int32)[None, :]).reshape(-1)
    order = jnp.arange(pieces, dtype=jnp.int32)
    earlier = (owner[:, None] == owner[None, :]) & (order[None, :] < order[:, None])
    target = owner * per_pair + jnp.sum(earlier.astype(jnp.int32), axis=1)

    got = []
    for at, count in chunks:
        send = filter_call(at, count, target, counts, start_vectors, conductance)
        if at == 0:
            coarse_in, local, target, send = lax.optimization_barrier((coarse_in, local, target, send))
        send = send.reshape(devices, per_pair, count * ROWS, ECELLS)
        arrived = lax.all_to_all(send, both, split_axis=0, concat_axis=0, tiled=True)
        got.append(arrived.reshape(pieces * count * ROWS, ECELLS))

    source = jnp.zeros(pieces, jnp.int32).at[target].set(local)
    ids = lax.all_to_all(source.reshape(devices, per_pair), both, split_axis=0, concat_axis=0, tiled=True).reshape(-1)

    near = packed_width(owned * bits)
    far = packed_width(per_pair * bits)
    out = whole(functools.partial(coarse_pack_kernel, groups), (groups, ROWS, near), coarse_in, name="coarse_pack")
    out = lax.all_to_all(out, "eight", split_axis=0, concat_axis=0, tiled=True)
    scratch = [pltpu.VMEM((hoods, width, vectors), jnp.float32), pltpu.SMEM((pieces,), jnp.int32)]
    out = whole(
        functools.partial(rows_kernel, per_pair),
        (devices, ROWS, far),
        target,
        out,
        scratch=scratch,
        prefetch=1,
        name="rows_out",
    )
    rows_in = lax.all_to_all(out, both, split_axis=0, concat_axis=0, tiled=True)

    cap = capacity.reshape(elements, 2, HALF // 2, HALF, HALF).transpose(0, 2, 3, 1, 4).reshape(elements, ECELLS) / ECELLS
    rows = 8 * slots
    phi = [pltpu.VMEM((elements * rows, ECELLS), jnp.float32)]
    sems = [pltpu.SemaphoreType.DMA((len(chunks),))]
    back = pl.pallas_call(
        functools.partial(applied_kernel, chunks, groups, per_pair),
        grid_spec=pltpu.PrefetchScalarGridSpec(
            num_scalar_prefetch=1,
            grid=(),
            in_specs=[VMEM, VMEM] + [ANY] * len(chunks),
            out_specs=VMEM,
            scratch_shapes=phi + [pltpu.VMEM((elements * rows, vectors), jnp.float32)] * 2 + sems,
        ),
        out_shape=jax.ShapeDtypeStruct((devices, ROWS, far), jnp.float32),
        name="applied",
    )(ids, rows_in, cap, *got)
    returned = lax.all_to_all(back, both, split_axis=0, concat_axis=0, tiled=True)
    galerkin = pl.pallas_call(
        functools.partial(galerkin_kernel, chunks, groups, per_pair),
        grid_spec=pltpu.PrefetchScalarGridSpec(
            num_scalar_prefetch=1,
            grid=(elements,),
            in_specs=[pl.BlockSpec((elements, ECELLS), lambda e, i: (0, 0))] + [ANY] * len(chunks),
            out_specs=pl.BlockSpec((1, rows, rows), lambda e, i: (e, 0, 0)),
            scratch_shapes=phi + sems,
        ),
        out_shape=jax.ShapeDtypeStruct((elements, rows, rows), jnp.float32),
        name="galerkin",
    )(ids, cap, *got)
    out = whole(
        functools.partial(sum_kernel, per_pair),
        (groups, ROWS, near),
        target,
        returned,
        scratch=scratch,
        prefetch=1,
        name="sum_octants",
    )
    out = lax.all_to_all(out, "eight", split_axis=0, concat_axis=0, tiled=True)
    coarse_out = whole(coarse_out_kernel, coarse_in.shape, out, name="coarse_out")
    return (galerkin, coarse_out)


def solution(mesh):
    in_specs = (
        P("wide", "eight", None),
        P("wide", None),
        P("wide"),
        P("wide", None),
        P(("wide", "eight"), None),
        P(("wide", "eight"), None, None),
    )
    out_specs = (P(("wide", "eight"), None, None), P(("wide", "eight"), None, None))
    return jax.shard_map(body, mesh=mesh, in_specs=in_specs, out_specs=out_specs, check_vma=False)
```

time: 501 us -> 294 us (0.59); the launches traced: 494 us -> 293 us
  other arithmetic: 137 us -> 2.14 us
  local copies, waits for them, and re-layouts: 135 us -> 8.64 us
  Pallas kernels: 0 us -> 99 us
  waiting for transfers between devices: 158 us -> 110 us
  blocking collectives: 6.85 us -> 51.2 us
  matrix products: 29.5 us -> 0 us
    pallas_call x0 -> x8, Pallas kernels: none -> 99 us  [the longest x2 54.5 us: filter_call(): pl.pallas_call(functools.partial(filter_kernel, first_slot, groups), grid...]
    sub x4 -> x0, other arithmetic: 87.3 us -> none  [filtered_basis(): 2.0 * (operate(current, diagonal, neighbour_links, plane_span) - centre *...]
    all_to_all x5, waiting for transfers between devices: 158 us -> 110 us  [the longest x2 107 us: body(): lax.all_to_all(send, both, split_axis=0, concat_axis=0, tiled=True)]
    all_to_all x1 -> x2, blocking collectives: 6.85 us -> 51.2 us  [the longest x1 25.8 us: body(): lax.all_to_all(back, both, split_axis=0, concat_axis=0, tiled=True)]
    mul x12 -> x0, local copies, waits for them, and re-layouts: 40 us -> none  [the longest x6 18.9 us: operate(): result = result - linked * moved]
    gather x7 -> x0, local copies, waits for them, and re-layouts: 34 us -> none  [the longest x1 23.2 us: body(): pieces[source_of].reshape(devices, per_pair, group_width, ECELLS)]
    dot_general x2 -> x0, matrix products: 29.5 us -> none  [the longest x1 21.5 us: body(): jnp.einsum('erc,esc->ers', weighted, basis_full, precision=lax.Precision....]
    transpose x1 -> x0, local copies, waits for them, and re-layouts: 23.3 us -> none  [octant_pieces(): cubic = jnp.transpose(cubic, axes_order)]
  transfers between devices with their start and end apart: 5 -> 5, of which waited for: 3 -> 4; matrix products, arithmetic and copies ran while one was open for 51% -> 1% of each run, Pallas kernels for 0% -> 18%
where the time goes in v1:
time: 294 us; the launch traced here: 293 us
  waiting for transfers between devices  110 us (37%)
  Pallas kernels  99 us (34%)
  blocking collectives  51.2 us (17%)
  starting transfers between devices  20.7 us (7%)
  local copies, waits for them, and re-layouts  8.64 us (3%)
    all_to_all x2, waiting for transfers between devices, body(): lax.all_to_all(send, both, split_axis=0, concat_axis=0, tiled=True)  107 us
    pallas_call x2, Pallas kernels, filter_call(): pl.pallas_call(functools.partial(filter_kernel, first_slot, groups), grid...  54.5 us
    all_to_all x1, blocking collectives, body(): lax.all_to_all(back, both, split_axis=0, concat_axis=0, tiled=True)  25.8 us
    all_to_all x1, blocking collectives, body(): rows_in = lax.all_to_all(out, both, split_axis=0, concat_axis=0, tiled=True)  25.5 us
    pallas_call x4, Pallas kernels, whole(): pl.pallas_call(f, grid_spec=pltpu.PrefetchScalarGridSpec(num_scalar_prefe...  15.8 us
    pallas_call x1, Pallas kernels, body(): pl.pallas_call(functools.partial(applied_kernel, chunks, groups, per_pair...  14.8 us
    pallas_call x1, Pallas kernels, body(): pl.pallas_call(functools.partial(galerkin_kernel, chunks, groups, per_pai...  14 us
    all_to_all x2, starting transfers between devices, body(): lax.all_to_all(send, both, split_axis=0, concat_axis=0, tiled=True)  7.77 us
  transfers between devices with their start and end apart: 5, of which 4 were waited for; matrix products, arithmetic and copies ran while one was open for 1% of the time, Pallas kernels for 18%

profile of v1, /device:TPU:0, one launch (start us, length us, event | category | flops | bytes accessed | tf_op | source)
XLA Modules:
  0.0 292.9 jit_solution(7517714011857054859)
XLA Ops:
  2.4 21.1 %filter0.1 = f32[128,8,512]{2,1,0:T(8,128)} custom-call(s32[128]{0:T(128)} %multiply_add_fusion.target_ref, s32[16]{0:T(128)} %counts_ref.3, bf16[16,24,4096]{2,1,0:T(8,128)(2,1)} %sv_ref.3, f32[16,4096]{1,0:T(8,128)} %cond_ref.3), custom_call_target="tpu_custom_call" | custom-call | tf_op jit(solution)/shard_map/filter0/pallas_call | solution.py:161
  23.6 0.8 copy.28.in_ref
  24.3 1.7 coarse_pack.1
  26.0 4.3 %all-to-all-start.3 = ((f32[4,8,768]{2,1,0:T(8,128)}), f32[4,8,768]{2,1,0:T(8,128)S(1)}, u32[]{:S(2)}, u32[]{:S(2)}) async-start(f32[4,8,768]{2,1,0:T(8,128)} %coarse_pack.1), calls=%async_computation.3 | async-start | bytes 196608 | tf_op jit(solution)/shard_map/all_to_all | solution.py:428
  30.3 1.0 scatter_custom_fusion
  32.0 2.6 all-to-all-done.3.in_ref
  34.6 5.4 %all-to-all-start = ((s32[32,1,4]{2,1,0:T(1,128)}), s32[32,1,4]{2,1,0:T(1,128)S(1)}, u32[]{:S(2)}, u32[]{:S(2)}) async-start(s32[32,1,4]{2,1,0:T(1,128)} %bitcast), calls=%async_computation | async-start | bytes 32768 | tf_op jit(solution)/shard_map/all_to_all | solution.py:423
  40.0 6.1 %rows_out.1 = f32[32,8,768]{2,1,0:T(8,128)} custom-call(s32[128]{0:T(128)} %multiply_add_fusion.target_ref, f32[4,8,768]{2,1,0:T(8,128)} %copy-done.1), custom_call_target="tpu_custom_call" | custom-call | tf_op jit(solution)/shard_map/rows_out/pallas_call | solution.py:380
  46.1 1.1 all-to-all-done
  47.1 25.5 %all_to_all.39.rows_in_ref = f32[32,8,768]{2,1,0:T(8,128)} all-to-all(f32[32,8,768]{2,1,0:T(8,128)} %rows_out.1), channel_id=1, replica_groups=mesh['wide'=8,'eight'=4] {'wide','eight'}, dimensions={0} | all-to-all | bytes 1572864 | tf_op jit(solution)/shard_map/all_to_all | solution.py:439
  72.6 3.6 %all-to-all-start.1 = ((f32[32,4,8,512]{3,2,1,0:T(8,128)}), f32[32,4,8,512]{3,2,1,0:T(8,128)S(1)}, u32[]{:S(2)}, u32[]{:S(2)}) async-start(f32[32,4,8,512]{3,2,1,0:T(8,128)} %bitcast.12), calls=%async_computation.1 | async-start | bytes 4194304 | tf_op jit(solution)/shard_map/all_to_all | solution.py:419
  76.2 33.4 %filter8.1 = f32[128,16,512]{2,1,0:T(8,128)} custom-call(s32[128]{0:T(128)} %multiply_add_fusion.target_ref, s32[16]{0:T(128)} %counts_ref.3, bf16[16,24,4096]{2,1,0:T(8,128)(2,1)} %sv_ref.3, f32[16,4096]{1,0:T(8,128)} %cond_ref.3), custom_call_target="tpu_custom_call" | custom-call | tf_op jit(solution)/shard_map/filter8/pallas_call | solution.py:161
  109.6 15.3 %all-to-all-done.1 = f32[32,4,8,512]{3,2,1,0:T(8,128)S(1)} async-done(((f32[32,4,8,512]{3,2,1,0:T(8,128)}), f32[32,4,8,512]{3,2,1,0:T(8,128)S(1)}, u32[]{:S(2)}, u32[]{:S(2)}) %all-to-all-start.1) | async-done | bytes 2097184 | tf_op jit(solution)/shard_map/all_to_all | solution.py:419
  125.0 1.3 copy-done
  126.3 4.1 %all-to-all-start.2 = ((f32[32,4,16,512]{3,2,1,0:T(8,128)}), f32[32,4,16,512]{3,2,1,0:T(8,128)}, u32[]{:S(2)}, u32[]{:S(2)}) async-start(f32[32,4,16,512]{3,2,1,0:T(8,128)} %bitcast.11), calls=%async_computation.2 | async-start | bytes 8388608 | tf_op jit(solution)/shard_map/all_to_all | solution.py:419
  130.7 0.8 div.32.cap_ref
  133.4 91.3 %all-to-all-done.2 = f32[32,4,16,512]{3,2,1,0:T(8,128)} async-done(((f32[32,4,16,512]{3,2,1,0:T(8,128)}), f32[32,4,16,512]{3,2,1,0:T(8,128)}, u32[]{:S(2)}, u32[]{:S(2)}) %all-to-all-start.2) | async-done | bytes 4194336 | tf_op jit(solution)/shard_map/all_to_all | solution.py:419
  224.7 14.8 %applied.1 = f32[32,8,768]{2,1,0:T(8,128)} custom-call(s32[128]{0:T(128)} %reshape.40.ids_ref, f32[32,8,768]{2,1,0:T(8,128)} %all_to_all.39.rows_in_ref, f32[4,512]{1,0:T(4,128)} %div.32.cap_ref, f32[1024,512]{1,0:T(8,128)} %bitcast.9, f32[2048,512]{1,0:T(8,128)} %bitcast.5.refs_1_), custom_call_target="tpu_custom_call" | custom-call | tf_op jit(solution)/shard_map/applied/pallas_call | solution.py:445
  239.4 25.8 %all_to_all.40.in_ref = f32[32,8,768]{2,1,0:T(8,128)} all-to-all(f32[32,8,768]{2,1,0:T(8,128)} %applied.1), channel_id=1, replica_groups=mesh['wide'=8,'eight'=4] {'wide','eight'}, dimensions={0} | all-to-all | bytes 1572864 | tf_op jit(solution)/shard_map/all_to_all | solution.py:457
  265.2 6.4 %sum_octants.1 = f32[4,8,768]{2,1,0:T(8,128)} custom-call(s32[128]{0:T(128)} %multiply_add_fusion.target_ref, f32[32,8,768]{2,1,0:T(8,128)} %all_to_all.40.in_ref), custom_call_target="tpu_custom_call" | custom-call | tf_op jit(solution)/shard_map/sum_octants/pallas_call | solution.py:380
  271.6 3.3 %all-to-all-start.6 = ((f32[4,8,768]{2,1,0:T(8,128)}), f32[4,8,768]{2,1,0:T(8,128)S(1)}, u32[]{:S(2)}, u32[]{:S(2)}) async-start(f32[4,8,768]{2,1,0:T(8,128)} %sum_octants.1), calls=%async_computation.6 | async-start | bytes 196608 | tf_op jit(solution)/shard_map/all_to_all | solution.py:479
  274.9 14.0 %galerkin.1 = f32[4,768,768]{2,1,0:T(8,128)} custom-call(s32[128]{0:T(128)} %reshape.40.ids_ref, f32[4,512]{1,0:T(4,128)} %div.32.cap_ref, f32[1024,512]{1,0:T(8,128)} %bitcast.10, f32[2048,512]{1,0:T(8,128)} %bitcast.5.refs_1_), custom_call_target="tpu_custom_call" | custom-call | tf_op jit(solution)/shard_map/galerkin/pallas_call | solution.py:458
  289.5 1.7 coarse_out.1
  291.2 1.7 copy.29
  (27 shorter events, 5.2 us)
Async XLA Ops:
  0.6 22.9 %copy-start.3 = (f32[4,96,64]{1,2,0:T(8,128)S(1)}, f32[4,96,64]{1,2,0:T(8,128)}, u32[]{:S(2)}) copy-start(f32[4,96,64]{1,2,0:T(8,128)} %param.11) | copy-start | bytes 294916
  2.3 28.0 %copy-start.4 = (s32[128]{0:T(128)S(1)}, s32[128]{0:T(128)}, u32[]{:S(2)}) copy-start(s32[128]{0:T(128)} %multiply_add_fusion.target_ref) | copy-start | bytes 1540
  26.0 8.6 %all-to-all-start.3 = ((f32[4,8,768]{2,1,0:T(8,128)}), f32[4,8,768]{2,1,0:T(8,128)S(1)}, u32[]{:S(2)}, u32[]{:S(2)}) async-start(f32[4,8,768]{2,1,0:T(8,128)} %coarse_pack.1), calls=%async_computation.3 | async-start | bytes 196608 | tf_op jit(solution)/shard_map/all_to_all | solution.py:428
  34.6 5.4 %copy-start.1 = (f32[4,8,768]{2,1,0:T(8,128)}, f32[4,8,768]{2,1,0:T(8,128)S(1)}, u32[]{:S(2)}) copy-start(f32[4,8,768]{2,1,0:T(8,128)S(1)} %all-to-all-done.3.in_ref) | copy-start | bytes 294916
  34.6 12.6 %all-to-all-start = ((s32[32,1,4]{2,1,0:T(1,128)}), s32[32,1,4]{2,1,0:T(1,128)S(1)}, u32[]{:S(2)}, u32[]{:S(2)}) async-start(s32[32,1,4]{2,1,0:T(1,128)} %bitcast), calls=%async_computation | async-start | bytes 32768 | tf_op jit(solution)/shard_map/all_to_all | solution.py:423
  72.6 52.3 %all-to-all-start.1 = ((f32[32,4,8,512]{3,2,1,0:T(8,128)}), f32[32,4,8,512]{3,2,1,0:T(8,128)S(1)}, u32[]{:S(2)}, u32[]{:S(2)}) async-start(f32[32,4,8,512]{3,2,1,0:T(8,128)} %bitcast.12), calls=%async_computation.1 | async-start | bytes 4194304 | tf_op jit(solution)/shard_map/all_to_all | solution.py:419
  125.0 1.3 copy-start
  125.0 5.5 %copy-start.5 = (f32[4,512]{1,0:T(4,128)S(1)}, f32[4,512]{1,0:T(4,128)}, u32[]{:S(2)}) copy-start(f32[4,512]{1,0:T(4,128)} %param.10) | copy-start | bytes 24580
  126.3 98.4 %all-to-all-start.2 = ((f32[32,4,16,512]{3,2,1,0:T(8,128)}), f32[32,4,16,512]{3,2,1,0:T(8,128)}, u32[]{:S(2)}, u32[]{:S(2)}) async-start(f32[32,4,16,512]{3,2,1,0:T(8,128)} %bitcast.11), calls=%async_computation.2 | async-start | bytes 8388608 | tf_op jit(solution)/shard_map/all_to_all | solution.py:419
  271.6 17.3 %all-to-all-start.6 = ((f32[4,8,768]{2,1,0:T(8,128)}), f32[4,8,768]{2,1,0:T(8,128)S(1)}, u32[]{:S(2)}, u32[]{:S(2)}) async-start(f32[4,8,768]{2,1,0:T(8,128)} %sum_octants.1), calls=%async_computation.6 | async-start | bytes 196608 | tf_op jit(solution)/shard_map/all_to_all | solution.py:479
  288.9 0.6 copy-start.2

commit v2 on v1

--- a/solution.py
+++ b/solution.py
@@ -16,7 +16,7 @@
 TILES = SIDE * SIDE * SIDE // LANES
 PAIR = SIDE * SIDE // LANES
 
-ANY = pl.BlockSpec(memory_space=pl.ANY)
+ANY = pl.BlockSpec(memory_space=pltpu.HBM)
 VMEM = pl.BlockSpec(memory_space=pltpu.VMEM)
 SMEM = pl.BlockSpec(memory_space=pltpu.SMEM)
 
@@ -195,64 +195,17 @@
     return (blocks + 1) // 2 * LANES
 
 
-def coarse_pack_kernel(groups, in_ref, out_ref):
-    owned, slots, _ = in_ref.shape
-    width = slots // groups
-    for e in range(groups):
-        blocks = [
-            in_ref[n, e * width + r : e * width + r + ROWS, :] for n in range(owned) for r in range(0, width, ROWS)
-        ]
-        for i, tile in enumerate(pack(blocks)):
-            out_ref[e, :, i * LANES : (i + 1) * LANES] = tile
-
-
-def rows_kernel(per_pair, target_ref, in_ref, out_ref, rows_ref, source_ref):
-    groups = in_ref.shape[0]
-    hoods, width, _ = rows_ref.shape
-    owned = hoods // groups
-    bits = width // ROWS
-    for e in range(groups):
-        for n in range(owned):
-            for r in range(bits):
-                k = n * bits + r
-                rows_ref[e * owned + n, r * ROWS : (r + 1) * ROWS, :] = half(
-                    in_ref[e, :, k // 2 * LANES : (k // 2 + 1) * LANES], k
-                )
-
-    def invert(p, carry):
-        source_ref[target_ref[p]] = p
-        return carry
-
-    lax.fori_loop(0, hoods * 8, invert, 0)
-
-    def place(d, carry):
-        blocks = []
-        for i in range(per_pair):
-            n = lax.div(source_ref[d * per_pair + i], 8)
-            blocks += [rows_ref[n, r * ROWS : (r + 1) * ROWS, :] for r in range(bits)]
-        for i, tile in enumerate(pack(blocks)):
-            out_ref[d, :, i * LANES : (i + 1) * LANES] = tile
-        return carry
-
-    lax.fori_loop(0, out_ref.shape[0], place, 0)
-
-
-def sum_kernel(per_pair, target_ref, in_ref, out_ref, rows_ref, source_ref):
+def sum_kernel(per_pair, source_ref, in_ref, after_ref, out_ref, rows_ref):
+    del after_ref
     groups = out_ref.shape[0]
     hoods, width, _ = rows_ref.shape
     owned = hoods // groups
     bits = width // ROWS
     rows_ref[...] = jnp.zeros_like(rows_ref)
 
-    def invert(p, carry):
-        source_ref[target_ref[p]] = p
-        return carry
-
-    lax.fori_loop(0, hoods * 8, invert, 0)
-
     def gather(d, carry):
         for i in range(per_pair):
-            n = lax.div(source_ref[d * per_pair + i], 8)
+            n = source_ref[d * per_pair + i]
             for r in range(bits):
                 k = i * bits + r
                 rows_ref[n, r * ROWS : (r + 1) * ROWS, :] += half(in_ref[d, :, k // 2 * LANES : (k // 2 + 1) * LANES], k)
@@ -269,16 +222,15 @@
 
 def coarse_out_kernel(in_ref, out_ref):
     groups = in_ref.shape[0]
-    owned, slots, _ = out_ref.shape
-    width = slots // groups
-    bits = width // ROWS
-    for e in range(groups):
-        for n in range(owned):
+    owned, _, slots = out_ref.shape
+    bits = slots // groups // ROWS
+    for n in range(owned):
+        rows = []
+        for e in range(groups):
             for r in range(bits):
                 k = n * bits + r
-                out_ref[n, e * width + r * ROWS : e * width + (r + 1) * ROWS, :] = half(
-                    in_ref[e, :, k // 2 * LANES : (k // 2 + 1) * LANES], k
-                )
+                rows.append(half(in_ref[e, :, k // 2 * LANES : (k // 2 + 1) * LANES], k))
+        out_ref[n] = jnp.transpose(jnp.concatenate(rows, axis=0))
 
 
 def split(x):
@@ -293,71 +245,68 @@
     return dot(xh, yh) + (dot(xh, yl) + dot(xl, yh))
 
 
-def gather_basis(chunks, groups, per_pair, ids_ref, got_refs, phi_ref, sems):
+def start_gather(chunks, groups, per_pair, e, from_ref, got_refs, phi_ref, sems):
     width = sum(count for _, count in chunks) * ROWS
-    stride = groups * width
-    pieces = ids_ref.shape[0]
-
-    def place(q, carry):
-        row = ids_ref[q] * stride + lax.rem(lax.div(q, per_pair), groups) * width
-        for k, (first, count) in enumerate(chunks):
-            rows = count * ROWS
-            pltpu.make_async_copy(
-                got_refs[k].at[pl.ds(pl.multiple_of(q * rows, ROWS), rows)],
-                phi_ref.at[pl.ds(pl.multiple_of(row + first, ROWS), rows)],
-                sems.at[k],
-            ).start()
-        return carry
-
-    lax.fori_loop(0, pieces, place, 0)
-    for k, (first, count) in enumerate(chunks):
-        pltpu.make_async_copy(got_refs[k], phi_ref.at[pl.ds(0, pieces * count * ROWS)], sems.at[k]).wait()
-
-
-def applied_kernel(chunks, groups, per_pair, ids_ref, rows_in_ref, cap_ref, *refs):
+    for o in range(8):
+        base = from_ref[e * 8 + o]
+        for g in range(groups):
+            q = base + g * per_pair
+            row = (e * 8 + o) * groups * width + g * width
+            for k, (first, count) in enumerate(chunks):
+                rows = count * ROWS
+                pltpu.make_async_copy(
+                    got_refs[k].at[pl.ds(pl.multiple_of(q * rows, ROWS), rows)],
+                    phi_ref.at[pl.ds(row + first, rows)],
+                    sems.at[e],
+                ).start()
+
+
+def wait_gather(e, rows, got_refs, phi_ref, sems):
+    pltpu.make_async_copy(
+        got_refs[-1].at[pl.ds(0, rows)], phi_ref.at[pl.ds(pl.multiple_of(e * rows, ROWS), rows)], sems.at[e]
+    ).wait()
+
+
+def applied_kernel(chunks, groups, per_pair, from_ref, hood_ref, key_ref, all_ref, cap_ref, *refs):
     got_refs = refs[: len(chunks)]
-    out_ref, phi_ref, r_ref, applied_ref, sems = refs[len(chunks) :]
+    out_ref, phi_ref, r_ref, applied_ref, sems, r_sems = refs[len(chunks) :]
     width = sum(count for _, count in chunks) * ROWS
     bits = width // ROWS
-    stride = groups * width
+    slots = groups * width
+    rows = 8 * slots
     elements = cap_ref.shape[0]
-    devices = rows_in_ref.shape[0]
-    gather_basis(chunks, groups, per_pair, ids_ref, got_refs, phi_ref, sems)
-
-    def row_of(s, i):
-        return ids_ref[s * per_pair + i] * stride + lax.rem(s, groups) * width
-
-    def place(s, carry):
-        for i in range(per_pair):
-            row = row_of(s, i)
-            for r in range(bits):
-                k = i * bits + r
-                r_ref[pl.ds(pl.multiple_of(row + r * ROWS, ROWS), ROWS), :] = half(
-                    rows_in_ref[s, :, k // 2 * LANES : (k // 2 + 1) * LANES], k
-                )
+    for e in range(elements):
+        for o in range(8):
+            k = e * 8 + o
+            pltpu.make_async_copy(all_ref.at[hood_ref[k]], r_ref.at[k], r_sems.at[e]).start()
+        start_gather(chunks, groups, per_pair, e, from_ref, got_refs, phi_ref, sems)
+    for e in range(elements):
+        pltpu.make_async_copy(all_ref.at[pl.ds(0, 8)], r_ref.at[pl.ds(e * 8, 8)], r_sems.at[e]).wait()
+        wait_gather(e, rows, got_refs, phi_ref, sems)
+        phi = split(phi_ref[e * rows : (e + 1) * rows, :])
+        sums = jnp.zeros((r_ref.shape[1], ECELLS), jnp.float32)
+        for o in range(8):
+            r = split(r_ref[e * 8 + o, :, :slots])
+            sums = sums + product(r, [x[o * slots : (o + 1) * slots] for x in phi], ((1,), (0,)))
+        sums = sums * cap_ref[e : e + 1, :]
+        applied_ref[e * rows : (e + 1) * rows, :] = product(phi, split(sums), ((1,), (1,)))
+
+    def back(w, carry):
+        keys = [key_ref[w * per_pair + i] * slots for i in range(per_pair)]
+        for g in range(groups):
+            blocks = []
+            for i in range(per_pair):
+                for r in range(bits):
+                    row = pl.multiple_of(keys[i] + (g * width + r * ROWS), ROWS)
+                    blocks.append(applied_ref[pl.ds(row, ROWS), :])
+            for i, tile in enumerate(pack(blocks)):
+                out_ref[w * groups + g, :, i * LANES : (i + 1) * LANES] = tile
         return carry
 
-    lax.fori_loop(0, devices, place, 0)
-    rows = 8 * stride
-    for e in range(elements):
-        phi = split(phi_ref[e * rows : (e + 1) * rows, :])
-        r = split(jnp.transpose(r_ref[e * rows : (e + 1) * rows, :]))
-        sums = product(r, phi, ((1,), (0,))) * cap_ref[e : e + 1, :]
-        applied_ref[e * rows : (e + 1) * rows, :] = product(phi, split(sums), ((1,), (1,)))
-
-    def back(s, carry):
-        blocks = []
-        for i in range(per_pair):
-            row = row_of(s, i)
-            blocks += [applied_ref[pl.ds(pl.multiple_of(row + r * ROWS, ROWS), ROWS), :] for r in range(bits)]
-        for i, tile in enumerate(pack(blocks)):
-            out_ref[s, :, i * LANES : (i + 1) * LANES] = tile
-        return carry
-
-    lax.fori_loop(0, devices, back, 0)
-
-
-def galerkin_kernel(chunks, groups, per_pair, ids_ref, cap_ref, *refs):
+    lax.fori_loop(0, out_ref.shape[0] // groups, back, 0)
+
+
+def galerkin_kernel(chunks, groups, per_pair, from_ref, cap_ref, *refs):
     got_refs = refs[: len(chunks)]
     out_ref, phi_ref, sems = refs[len(chunks) :]
     width = sum(count for _, count in chunks) * ROWS
@@ -366,8 +315,10 @@
 
     @pl.when(e == 0)
     def _():
-        gather_basis(chunks, groups, per_pair, ids_ref, got_refs, phi_ref, sems)
-
+        for i in range(cap_ref.shape[0]):
+            start_gather(chunks, groups, per_pair, i, from_ref, got_refs, phi_ref, sems)
+
+    wait_gather(e, rows, got_refs, phi_ref, sems)
     phi = phi_ref[pl.ds(pl.multiple_of(e * rows, ROWS), rows), :]
     weighted = phi * cap_ref[pl.ds(e, 1), :]
     out_ref[0] = product(split(weighted), split(phi), ((1,), (1,)))
@@ -376,24 +327,35 @@
 CHUNKS = ((0, 1), (8, 2))
 
 
-def whole(f, shape, *args, scratch=(), prefetch=0, name=None):
-    return pl.pallas_call(
-        f,
-        grid_spec=pltpu.PrefetchScalarGridSpec(
-            num_scalar_prefetch=prefetch,
-            grid=(),
-            in_specs=[VMEM] * (len(args) - prefetch),
-            out_specs=VMEM,
-            scratch_shapes=list(scratch),
-        ),
-        out_shape=jax.ShapeDtypeStruct(shape, jnp.float32),
-        name=name,
-    )(*args)
+def exchange_steps(wide, groups):
+    steps = []
+    for axis, size in (("wide", wide), ("eight", groups)):
+        distance = size // 2
+        while distance:
+            steps.append((axis, size, distance))
+            distance //= 2
+    return steps
+
+
+def gather_all(x, steps):
+    for axis, size, distance in steps:
+        there = lax.ppermute(x, axis, [(i, i ^ distance) for i in range(size)])
+        x = jnp.concatenate([x, there], axis=0)
+    return x
+
+
+def block_of(steps, wide_at, eight_at):
+    at = {"wide": wide_at ^ lax.axis_index("wide"), "eight": eight_at ^ lax.axis_index("eight")}
+    block = 0
+    for k, (axis, _, distance) in enumerate(steps):
+        block = block + jnp.where(at[axis] & distance, 1 << k, 0)
+    return block
 
 
 def body(start_vectors, conductance, counts, element_of, capacity, coarse_in):
     groups = lax.axis_size("eight")
-    devices = lax.axis_size("wide") * groups
+    wide = lax.axis_size("wide")
+    devices = wide * groups
     hoods, width, cells = start_vectors.shape
     owned = hoods // groups
     elements = capacity.shape[0]
@@ -403,57 +365,72 @@
     bits = width // ROWS
     chunks = CHUNKS
     both = ("wide", "eight")
+    ints = jnp.int32
 
     owner = (element_of // elements).reshape(-1)
-    local = (element_of % elements * 8 + jnp.arange(8, dtype=jnp.int32)[None, :]).reshape(-1)
-    order = jnp.arange(pieces, dtype=jnp.int32)
+    order = jnp.arange(pieces, dtype=ints)
     earlier = (owner[:, None] == owner[None, :]) & (order[None, :] < order[:, None])
-    target = owner * per_pair + jnp.sum(earlier.astype(jnp.int32), axis=1)
+    target = owner * per_pair + jnp.sum(earlier.astype(ints), axis=1)
 
     got = []
+    held = (coarse_in, element_of, capacity, target)
     for at, count in chunks:
         send = filter_call(at, count, target, counts, start_vectors, conductance)
-        if at == 0:
-            coarse_in, local, target, send = lax.optimization_barrier((coarse_in, local, target, send))
+        held, send = lax.optimization_barrier((held, send))
         send = send.reshape(devices, per_pair, count * ROWS, ECELLS)
         arrived = lax.all_to_all(send, both, split_axis=0, concat_axis=0, tiled=True)
         got.append(arrived.reshape(pieces * count * ROWS, ECELLS))
-
-    source = jnp.zeros(pieces, jnp.int32).at[target].set(local)
-    ids = lax.all_to_all(source.reshape(devices, per_pair), both, split_axis=0, concat_axis=0, tiled=True).reshape(-1)
+    coarse_in, element_of, capacity, late_target = held
+
+    steps = exchange_steps(wide, groups)
+    own = lax.dynamic_slice_in_dim(element_of, lax.axis_index("eight") * owned, owned, axis=0)
+    margin = jnp.zeros((owned, vectors, LANES - slots), jnp.float32).at[:, 0, :8].set(own.astype(jnp.float32))
+    every = gather_all(jnp.concatenate([jnp.swapaxes(coarse_in, 1, 2), margin], axis=2), steps)
+
+    wide_at = jnp.arange(wide, dtype=ints)[:, None]
+    eight_at = jnp.arange(groups, dtype=ints)[None, :]
+    block = block_of(steps, wide_at, eight_at)
+    incidence = every[:, 0, slots : slots + 8].reshape(devices, owned * 8)[block.reshape(-1)]
+    incidence = incidence.astype(ints).reshape(wide, pieces)
+    me = lax.axis_index("wide") * groups + lax.axis_index("eight")
+    mine = incidence // elements == me
+    before = (order[:, None] < order[None, :]).astype(jnp.float32)
+    rank = jnp.dot(mine.astype(jnp.float32), before).astype(ints)
+    key = incidence % elements * 8 + order[None, :] % 8
+    hood = (block[:, :, None] * owned + jnp.arange(owned, dtype=ints)).reshape(wide, hoods)
+    hood = jnp.broadcast_to(hood[:, :, None], (wide, hoods, 8)).reshape(wide, pieces)
+    first = wide_at * (groups * per_pair) + rank
+    chosen = mine[None] & (key[None] == jnp.arange(elements * 8, dtype=ints)[:, None, None])
+    from_at = jnp.sum(jnp.where(chosen, first[None], 0), axis=(1, 2))
+    hood_at = jnp.sum(jnp.where(chosen, hood[None], 0), axis=(1, 2))
+    placed = mine[:, None, :] & (rank[:, None, :] == jnp.arange(per_pair, dtype=ints)[None, :, None])
+    key_at = jnp.sum(jnp.where(placed, key[:, None, :], 0), axis=2).reshape(-1)
+    hit = late_target[None, :] == order[:, None]
+    source = jnp.sum(jnp.where(hit, order[None, :] // 8, 0), axis=1)
 
     near = packed_width(owned * bits)
     far = packed_width(per_pair * bits)
-    out = whole(functools.partial(coarse_pack_kernel, groups), (groups, ROWS, near), coarse_in, name="coarse_pack")
-    out = lax.all_to_all(out, "eight", split_axis=0, concat_axis=0, tiled=True)
-    scratch = [pltpu.VMEM((hoods, width, vectors), jnp.float32), pltpu.SMEM((pieces,), jnp.int32)]
-    out = whole(
-        functools.partial(rows_kernel, per_pair),
-        (devices, ROWS, far),
-        target,
-        out,
-        scratch=scratch,
-        prefetch=1,
-        name="rows_out",
-    )
-    rows_in = lax.all_to_all(out, both, split_axis=0, concat_axis=0, tiled=True)
-
     cap = capacity.reshape(elements, 2, HALF // 2, HALF, HALF).transpose(0, 2, 3, 1, 4).reshape(elements, ECELLS) / ECELLS
     rows = 8 * slots
     phi = [pltpu.VMEM((elements * rows, ECELLS), jnp.float32)]
-    sems = [pltpu.SemaphoreType.DMA((len(chunks),))]
+    sems = [pltpu.SemaphoreType.DMA((elements,))]
     back = pl.pallas_call(
         functools.partial(applied_kernel, chunks, groups, per_pair),
         grid_spec=pltpu.PrefetchScalarGridSpec(
-            num_scalar_prefetch=1,
+            num_scalar_prefetch=3,
             grid=(),
-            in_specs=[VMEM, VMEM] + [ANY] * len(chunks),
+            in_specs=[ANY, VMEM] + [ANY] * len(chunks),
             out_specs=VMEM,
-            scratch_shapes=phi + [pltpu.VMEM((elements * rows, vectors), jnp.float32)] * 2 + sems,
+            scratch_shapes=phi
+            + [
+                pltpu.VMEM((elements * 8, vectors, LANES), jnp.float32),
+                pltpu.VMEM((elements * rows, vectors), jnp.float32),
+            ]
+            + sems * 2,
         ),
         out_shape=jax.ShapeDtypeStruct((devices, ROWS, far), jnp.float32),
         name="applied",
-    )(ids, rows_in, cap, *got)
+    )(from_at, hood_at, key_at, every, cap, *got)
     returned = lax.all_to_all(back, both, split_axis=0, concat_axis=0, tiled=True)
     galerkin = pl.pallas_call(
         functools.partial(galerkin_kernel, chunks, groups, per_pair),
@@ -466,19 +443,28 @@
         ),
         out_shape=jax.ShapeDtypeStruct((elements, rows, rows), jnp.float32),
         name="galerkin",
-    )(ids, cap, *got)
-    out = whole(
+    )(from_at, cap, *got)
+    out = pl.pallas_call(
         functools.partial(sum_kernel, per_pair),
-        (groups, ROWS, near),
-        target,
-        returned,
-        scratch=scratch,
-        prefetch=1,
+        grid_spec=pltpu.PrefetchScalarGridSpec(
+            num_scalar_prefetch=1,
+            grid=(),
+            in_specs=[VMEM, ANY],
+            out_specs=VMEM,
+            scratch_shapes=[pltpu.VMEM((hoods, width, vectors), jnp.float32)],
+        ),
+        out_shape=jax.ShapeDtypeStruct((groups, ROWS, near), jnp.float32),
         name="sum_octants",
-    )
+    )(source, returned, galerkin)
     out = lax.all_to_all(out, "eight", split_axis=0, concat_axis=0, tiled=True)
-    coarse_out = whole(coarse_out_kernel, coarse_in.shape, out, name="coarse_out")
-    return (galerkin, coarse_out)
+    coarse_out = pl.pallas_call(
+        coarse_out_kernel,
+        in_specs=[VMEM],
+        out_specs=VMEM,
+        out_shape=jax.ShapeDtypeStruct((owned, vectors, slots), jnp.float32),
+        name="coarse_out",
+    )(out)
+    return (galerkin, jnp.swapaxes(coarse_out, 1, 2))
 
 
 def solution(mesh):

time: 294 us -> 299 us (1.017)
  waiting for transfers between devices: 110 us -> 159 us
  blocking collectives: 51.2 us -> 8.28 us
  Pallas kernels: 99 us -> 88 us
  local copies, waits for them, and re-layouts: 8.64 us -> 13.1 us
  other arithmetic: 2.14 us -> 5.42 us
    ppermute x0 -> x5, waiting for transfers between devices: none -> 136 us  [gather_all(): there = lax.ppermute(x, axis, [(i, i ^ distance) for i in range(size)])]
    all_to_all x2, waiting for transfers between devices: 107 us -> 15.3 us  [body(): lax.all_to_all(send, both, split_axis=0, concat_axis=0, tiled=True)]
    all_to_all x2 -> x1, blocking collectives: 51.2 us -> 8.28 us  [body(): out = lax.all_to_all(out, 'eight', split_axis=0, concat_axis=0, tiled=True)]
    pallas_call x4 -> x2, Pallas kernels: 15.8 us -> 6.95 us  [the longest x1 5.15 us: body(): pl.pallas_call(functools.partial(sum_kernel, per_pair), grid_spec=pltpu.P...]
    all_to_all x3 -> x1, starting transfers between devices: 13 us -> 6.61 us  [body(): lax.all_to_all(back, both, split_axis=0, concat_axis=0, tiled=True)]
    ppermute x0 -> x5, starting transfers between devices: none -> 4.79 us  [gather_all(): there = lax.ppermute(x, axis, [(i, i ^ distance) for i in range(size)])]
    all_to_all x2, starting transfers between devices: 7.77 us -> 11.7 us  [body(): lax.all_to_all(send, both, split_axis=0, concat_axis=0, tiled=True)]
    all_to_all x3 -> x1, waiting for transfers between devices: 3.66 us -> 7.43 us  [body(): lax.all_to_all(back, both, split_axis=0, concat_axis=0, tiled=True)]
  transfers between devices with their start and end apart: 5 -> 8, of which waited for: 4 -> 7; matrix products, arithmetic and copies ran while one was open for 1% -> 5% of each run, Pallas kernels for 18% -> 15%
where the time goes in v2:
time: 299 us; the launch traced here: 298 us
  waiting for transfers between devices  159 us (53%)
  Pallas kernels  88 us (29%)
  starting transfers between devices  23.1 us (8%)
  local copies, waits for them, and re-layouts  13.1 us (4%)
  blocking collectives  8.28 us (3%)
  other arithmetic  5.42 us (2%)
    ppermute x5, waiting for transfers between devices, gather_all(): there = lax.ppermute(x, axis, [(i, i ^ distance) for i in range(size)])  136 us
    pallas_call x2, Pallas kernels, filter_call(): pl.pallas_call(functools.partial(filter_kernel, first_slot, groups), grid...  54.5 us
    all_to_all x2, waiting for transfers between devices, body(): lax.all_to_all(send, both, split_axis=0, concat_axis=0, tiled=True)  15.3 us
    pallas_call x1, Pallas kernels, body(): pl.pallas_call(functools.partial(applied_kernel, chunks, groups, per_pair...  14.2 us
    pallas_call x1, Pallas kernels, body(): pl.pallas_call(functools.partial(galerkin_kernel, chunks, groups, per_pai...  12.4 us
    all_to_all x2, starting transfers between devices, body(): lax.all_to_all(send, both, split_axis=0, concat_axis=0, tiled=True)  11.7 us
    all_to_all x1, blocking collectives, body(): out = lax.all_to_all(out, 'eight', split_axis=0, concat_axis=0, tiled=True)  8.28 us
    all_to_all x1, waiting for transfers between devices, body(): lax.all_to_all(back, both, split_axis=0, concat_axis=0, tiled=True)  7.43 us
  transfers between devices with their start and end apart: 8, of which 7 were waited for; matrix products, arithmetic and copies ran while one was open for 5% of the time, Pallas kernels for 15%

profile of v2, /device:TPU:0, one launch (start us, length us, event | category | flops | bytes accessed | tf_op | source)
XLA Modules:
  0.0 298.0 jit_solution(3818737340893092292)
XLA Ops:
  2.2 21.1 %filter0.1 = f32[128,8,512]{2,1,0:T(8,128)} custom-call(s32[128]{0:T(128)} %multiply_add_fusion.target_ref, s32[16]{0:T(128)} %counts_ref.3, bf16[16,24,4096]{2,1,0:T(8,128)(2,1)} %sv_ref.3, f32[16,4096]{1,0:T(8,128)} %cond_ref.3), custom_call_target="tpu_custom_call" | custom-call | tf_op jit(solution)/shard_map/filter0/pallas_call | solution.py:161
  23.3 7.3 %all-to-all-start = ((f32[32,4,8,512]{3,2,1,0:T(8,128)}), f32[32,4,8,512]{3,2,1,0:T(8,128)S(1)}, u32[]{:S(2)}, u32[]{:S(2)}) async-start(f32[32,4,8,512]{3,2,1,0:T(8,128)} %bitcast.18), calls=%async_computation | async-start | bytes 4194304 | tf_op jit(solution)/shard_map/all_to_all | solution.py:381
  30.6 33.4 %filter8.1 = f32[128,16,512]{2,1,0:T(8,128)} custom-call(s32[128]{0:T(128)} %multiply_add_fusion.target_ref, s32[16]{0:T(128)} %counts_ref.3, bf16[16,24,4096]{2,1,0:T(8,128)(2,1)} %sv_ref.3, f32[16,4096]{1,0:T(8,128)} %cond_ref.3), custom_call_target="tpu_custom_call" | custom-call | tf_op jit(solution)/shard_map/filter8/pallas_call | solution.py:161
  64.0 15.3 %all-to-all-done = f32[32,4,8,512]{3,2,1,0:T(8,128)S(1)} async-done(((f32[32,4,8,512]{3,2,1,0:T(8,128)}), f32[32,4,8,512]{3,2,1,0:T(8,128)S(1)}, u32[]{:S(2)}, u32[]{:S(2)}) %all-to-all-start) | async-done | bytes 2097184 | tf_op jit(solution)/shard_map/all_to_all | solution.py:381
  79.3 1.4 copy-done
  80.7 4.3 %all-to-all-start.1 = ((f32[32,4,16,512]{3,2,1,0:T(8,128)}), f32[32,4,16,512]{3,2,1,0:T(8,128)}, u32[]{:S(2)}, u32[]{:S(2)}) async-start(f32[32,4,16,512]{3,2,1,0:T(8,128)} %bitcast.17), calls=%async_computation.1 | async-start | bytes 8388608 | tf_op jit(solution)/shard_map/all_to_all | solution.py:381
  86.0 2.4 collective-permute-start
  88.4 96.2 %collective-permute-done = f32[4,64,128]{2,1,0:T(8,128)S(1)} collective-permute-done((f32[4,64,128]{2,1,0:T(8,128)S(1)}, f32[4,64,128]{2,1,0:T(8,128)S(1)}, u32[]{:S(2)}, u32[]{:S(2)}) %collective-permute-start) | collective-permute-done | bytes 131104 | tf_op jit(solution)/shard_map/ppermute | solution.py:342
  184.8 7.7 %collective-permute-done.1 = f32[8,64,128]{2,1,0:T(8,128)S(1)} collective-permute-done((f32[8,64,128]{2,1,0:T(8,128)S(1)}, f32[8,64,128]{2,1,0:T(8,128)S(1)}, u32[]{:S(2)}, u32[]{:S(2)}) %collective-permute-start.1) | collective-permute-done | bytes 262176 | tf_op jit(solution)/shard_map/ppermute | solution.py:342
  192.7 1.3 collective-permute-start.2
  194.0 11.2 %collective-permute-done.2 = f32[16,64,128]{2,1,0:T(8,128)S(1)} collective-permute-done((f32[16,64,128]{2,1,0:T(8,128)S(1)}, f32[16,64,128]{2,1,0:T(8,128)S(1)}, u32[]{:S(2)}, u32[]{:S(2)}) %collective-permute-start.2) | collective-permute-done | bytes 524320 | tf_op jit(solution)/shard_map/ppermute | solution.py:342
  209.7 18.7 %collective-permute-done.3 = f32[32,64,128]{2,1,0:T(8,128)S(1)} collective-permute-done((f32[32,64,128]{2,1,0:T(8,128)S(1)}, f32[32,64,128]{2,1,0:T(8,128)S(1)}, u32[]{:S(2)}, u32[]{:S(2)}) %collective-permute-start.3) | collective-permute-done | bytes 1048608 | tf_op jit(solution)/shard_map/ppermute | solution.py:342
  228.3 1.6 constant_dynamic-update-slice_fusion
  231.7 2.6 collective-permute-done.4
  234.3 1.5 constant_dynamic-update-slice_fusion.5.all_ref
  235.7 1.3 slice_reduce_fusion
  238.8 1.8 select_reduce_fusion
  240.5 14.2 %applied.1 = f32[32,8,768]{2,1,0:T(8,128)} custom-call(s32[32]{0:T(128)} %get-tuple-element.35.from_ref, s32[32]{0:T(128)} %get-tuple-element.34.hood_ref, s32[32]{0:T(128)} %reshape.380.key_ref, f32[128,64,128]{2,1,0:T(8,128)} %constant_dynamic-update-slice_fusion.5.all_ref, f32[4,512]{1,0:T(4,128)} %div.56.cap_ref, f32[1024,512]{1,0:T(8,128)} %bitcast.15, ...), custom_call_target="tpu_custom_call" | custom-call | tf_op jit(solution)/shard_map/applied/pallas_call | solution.py:417
  254.7 6.6 %all-to-all-start.2 = ((f32[32,8,768]{2,1,0:T(8,128)}), f32[32,8,768]{2,1,0:T(8,128)S(1)}, u32[]{:S(2)}, u32[]{:S(2)}) async-start(f32[32,8,768]{2,1,0:T(8,128)} %applied.1), calls=%async_computation.2 | async-start | bytes 1572864 | tf_op jit(solution)/shard_map/all_to_all | solution.py:434
  262.1 12.4 %galerkin.1.after_ref = f32[4,768,768]{2,1,0:T(8,128)} custom-call(s32[32]{0:T(128)} %get-tuple-element.35.from_ref, f32[4,512]{1,0:T(4,128)} %div.56.cap_ref, f32[1024,512]{1,0:T(8,128)} %bitcast.16, f32[2048,512]{1,0:T(8,128)} %bitcast.7.refs_1_), custom_call_target="tpu_custom_call" | custom-call | tf_op jit(solution)/shard_map/galerkin/pallas_call | solution.py:435
  274.5 7.4 %all-to-all-done.2.in_ref = f32[32,8,768]{2,1,0:T(8,128)S(1)} async-done(((f32[32,8,768]{2,1,0:T(8,128)}), f32[32,8,768]{2,1,0:T(8,128)S(1)}, u32[]{:S(2)}, u32[]{:S(2)}) %all-to-all-start.2) | async-done | bytes 786464 | tf_op jit(solution)/shard_map/all_to_all | solution.py:434
  282.8 5.2 %sum_octants.1 = f32[4,8,768]{2,1,0:T(8,128)} custom-call(s32[128]{0:T(128)} %select_reduce_fusion.2.source_ref, f32[32,8,768]{2,1,0:T(8,128)} %copy-done.1, f32[4,768,768]{2,1,0:T(8,128)} %galerkin.1.after_ref), custom_call_target="tpu_custom_call" | custom-call | tf_op jit(solution)/shard_map/sum_octants/pallas_call | solution.py:447
  288.0 8.3 %all_to_all.20.in_ref = f32[4,8,768]{2,1,0:T(8,128)} all-to-all(f32[4,8,768]{2,1,0:T(8,128)} %sum_octants.1), channel_id=1, replica_groups=mesh['wide'=8,'eight'=4] {'eight'}, dimensions={0} | all-to-all | bytes 196608 | tf_op jit(solution)/shard_map/all_to_all | solution.py:459
  296.2 1.8 coarse_out.1
  (63 shorter events, 12.2 us)
Async XLA Ops:
  23.3 56.1 %all-to-all-start = ((f32[32,4,8,512]{3,2,1,0:T(8,128)}), f32[32,4,8,512]{3,2,1,0:T(8,128)S(1)}, u32[]{:S(2)}, u32[]{:S(2)}) async-start(f32[32,4,8,512]{3,2,1,0:T(8,128)} %bitcast.18), calls=%async_computation | async-start | bytes 4194304 | tf_op jit(solution)/shard_map/all_to_all | solution.py:381
  79.3 1.4 copy-start
  79.3 5.7 %copy-start.3 = (s32[16,8]{0,1:T(8,128)S(1)}, s32[16,8]{0,1:T(8,128)}, u32[]{:S(2)}) copy-start(s32[16,8]{0,1:T(8,128)} %param.11) | copy-start | bytes 1540
  79.3 5.9 %copy-start.2 = (f32[4,96,64]{1,2,0:T(8,128)S(1)}, f32[4,96,64]{1,2,0:T(8,128)}, u32[]{:S(2)}) copy-start(f32[4,96,64]{1,2,0:T(8,128)} %param.13) | copy-start | bytes 294916
  80.7 159.8 %all-to-all-start.1 = ((f32[32,4,16,512]{3,2,1,0:T(8,128)}), f32[32,4,16,512]{3,2,1,0:T(8,128)}, u32[]{:S(2)}, u32[]{:S(2)}) async-start(f32[32,4,16,512]{3,2,1,0:T(8,128)} %bitcast.17), calls=%async_computation.1 | async-start | bytes 8388608 | tf_op jit(solution)/shard_map/all_to_all | solution.py:381
  86.0 98.6 %collective-permute-start = (f32[4,64,128]{2,1,0:T(8,128)S(1)}, f32[4,64,128]{2,1,0:T(8,128)S(1)}, u32[]{:S(2)}, u32[]{:S(2)}) collective-permute-start(f32[4,64,128]{2,1,0:T(8,128)S(1)} %get-tuple-element.37), channel_id=1, source_target_pairs={{0,16},{4,20},{8,24},{12,28},{16,0},{20,4},{24,8},{28,12},{1,17},{... | collective-permute-start | bytes 393224 | tf_op jit(solution)/shard_map/ppermute | solution.py:342
  184.7 7.8 %collective-permute-start.1 = (f32[8,64,128]{2,1,0:T(8,128)S(1)}, f32[8,64,128]{2,1,0:T(8,128)S(1)}, u32[]{:S(2)}, u32[]{:S(2)}) collective-permute-start(f32[8,64,128]{2,1,0:T(8,128)S(1)} %pad_maximum_fusion.2), channel_id=1, source_target_pairs={{0,8},{4,12},{8,0},{12,4},{16,24},{20,28},{24,16},{28,20},{1,9},{5... | collective-permute-start | bytes 786440 | tf_op jit(solution)/shard_map/ppermute | solution.py:342
  192.6 38.0 %copy-start.4 = (f32[4,512]{1,0:T(4,128)S(1)}, f32[4,512]{1,0:T(4,128)}, u32[]{:S(2)}) copy-start(f32[4,512]{1,0:T(4,128)} %param.12) | copy-start | bytes 24580
  192.7 12.6 %collective-permute-start.2 = (f32[16,64,128]{2,1,0:T(8,128)S(1)}, f32[16,64,128]{2,1,0:T(8,128)S(1)}, u32[]{:S(2)}, u32[]{:S(2)}) collective-permute-start(f32[16,64,128]{2,1,0:T(8,128)S(1)} %pad_maximum_fusion.1), channel_id=1, source_target_pairs={{0,4},{4,0},{8,12},{12,8},{16,20},{20,16},{24,28},{28,24},{1,5},{5... | collective-permute-start | bytes 1572872 | tf_op jit(solution)/shard_map/ppermute | solution.py:342
  205.4 23.0 %collective-permute-start.3 = (f32[32,64,128]{2,1,0:T(8,128)S(1)}, f32[32,64,128]{2,1,0:T(8,128)S(1)}, u32[]{:S(2)}, u32[]{:S(2)}) collective-permute-start(f32[32,64,128]{2,1,0:T(8,128)S(1)} %pad_maximum_fusion), channel_id=1, source_target_pairs={{0,2},{1,3},{2,0},{3,1},{4,6},{5,7},{6,4},{7,5},{8,10},{9,11},{10,... | collective-permute-start | bytes 3145736 | tf_op jit(solution)/shard_map/ppermute | solution.py:342
  229.9 4.4 %collective-permute-start.4 = (f32[64,64,128]{2,1,0:T(8,128)}, f32[64,64,128]{2,1,0:T(8,128)S(1)}, u32[]{:S(2)}, u32[]{:S(2)}) collective-permute-start(f32[64,64,128]{2,1,0:T(8,128)} %get-tuple-element.38), channel_id=1, source_target_pairs={{0,1},{1,0},{2,3},{3,2},{4,5},{5,4},{6,7},{7,6},{8,9},{9,8},{10,11... | collective-permute-start | bytes 6291464 | tf_op jit(solution)/shard_map/ppermute | solution.py:342
  240.5 20.8 %copy-start.5 = (s32[128]{0:T(128)S(1)}, s32[128]{0:T(128)}, u32[]{:S(2)}) copy-start(s32[128]{0:T(128)} %multiply_add_fusion.target_ref) | copy-start | bytes 1540
  254.7 27.2 %all-to-all-start.2 = ((f32[32,8,768]{2,1,0:T(8,128)}), f32[32,8,768]{2,1,0:T(8,128)S(1)}, u32[]{:S(2)}, u32[]{:S(2)}) async-start(f32[32,8,768]{2,1,0:T(8,128)} %applied.1), calls=%async_computation.2 | async-start | bytes 1572864 | tf_op jit(solution)/shard_map/all_to_all | solution.py:434
  281.9 0.9 copy-start.1

commit v3 on v2

--- a/solution.py
+++ b/solution.py
@@ -46,7 +46,9 @@
             w_ref[i, t] = values[:, t * LANES : (t + 1) * LANES]
 
 
-def filter_kernel(first_slot, groups, target_ref, counts_ref, sv_ref, cond_ref, send_ref, w_ref, y_ref, out_ref, sems):
+def filter_kernel(first_slot, groups, per_pair, extra, *refs):
+    target_ref, counts_ref, source_ref, sv_ref, cond_ref = refs[:5]
+    extra_refs, (send_ref, w_ref, y_ref, out_ref, sems, more_ref, more_sem) = refs[5:-7], refs[-7:]
     n = pl.program_id(0)
     last = pl.num_programs(0) - 1
     rows = groups * ROWS
@@ -111,7 +113,9 @@
     slot = lax.rem(n, 2)
 
     def copy_out(step_slot, piece, o):
-        return pltpu.make_async_copy(out_ref.at[step_slot, o], send_ref.at[piece], sems.at[step_slot, o])
+        at = pl.multiple_of(lax.rem(piece, per_pair) * 4 * rows, ROWS)
+        place = send_ref.at[lax.div(piece, per_pair), pl.ds(at, 4 * rows)]
+        return pltpu.make_async_copy(out_ref.at[step_slot, o], place, sems.at[step_slot, o])
 
     @pl.when(n >= 2)
     def _():
@@ -143,41 +147,51 @@
                     near = jnp.where(even, pair[0], pltpu.roll(pair[1], HALF, 1))
                     far = jnp.where(even, pltpu.roll(pair[0], LANES - HALF, 1), pair[1])
                     for dz, value in enumerate((near, far)):
-                        out_ref[slot, dx * 4 + d * 2 + dz, g * ROWS : (g + 1) * ROWS, p * LANES : (p + 1) * LANES] = value
+                        at = p * rows + g * ROWS
+                        out_ref[slot, dx * 4 + d * 2 + dz, at : at + ROWS, :] = value
     for o in range(8):
         copy_out(slot, target_ref[n * 8 + o], o).start()
 
     @pl.when(n == last)
     def _():
+        extra(per_pair, source_ref, *extra_refs, more_ref)
+        base = per_pair * 4 * rows
+        more = pltpu.make_async_copy(more_ref, send_ref.at[:, pl.ds(base, more_ref.shape[1])], more_sem)
+        more.start()
+        more.wait()
         for o in range(8):
             copy_out(1 - slot, 0, o).wait()
         for o in range(8):
             copy_out(slot, 0, o).wait()
 
 
-def filter_call(first_slot, groups, target, counts, start_vectors, conductance):
+def filter_call(first_slot, groups, devices, target, counts, source, start_vectors, conductance, extra, more_rows, more=()):
     hoods, width, cells = start_vectors.shape
     rows = groups * ROWS
+    per_pair = hoods * 8 // devices
     return pl.pallas_call(
-        functools.partial(filter_kernel, first_slot, groups),
+        functools.partial(filter_kernel, first_slot, groups, per_pair, extra),
         grid_spec=pltpu.PrefetchScalarGridSpec(
-            num_scalar_prefetch=2,
+            num_scalar_prefetch=3,
             grid=(hoods,),
             in_specs=[
-                pl.BlockSpec((1, width, cells), lambda n, t, c: (n, 0, 0)),
-                pl.BlockSpec((hoods, cells), lambda n, t, c: (0, 0)),
-            ],
+                pl.BlockSpec((1, width, cells), lambda n, *_: (n, 0, 0)),
+                pl.BlockSpec((hoods, cells), lambda n, *_: (0, 0)),
+            ]
+            + [pl.BlockSpec(x.shape, lambda n, *_, k=x.ndim: (0,) * k) for x in more],
             out_specs=ANY,
             scratch_shapes=[
                 pltpu.VMEM((7, TILES, hoods, LANES), jnp.float32),
                 pltpu.VMEM((3, groups, ROWS, cells), jnp.float32),
-                pltpu.VMEM((2, 8, rows, ECELLS), jnp.float32),
+                pltpu.VMEM((2, 8, 4 * rows, LANES), jnp.float32),
                 pltpu.SemaphoreType.DMA((2, 8)),
+                pltpu.VMEM((devices, more_rows, LANES), jnp.float32),
+                pltpu.SemaphoreType.DMA,
             ],
         ),
-        out_shape=jax.ShapeDtypeStruct((hoods * 8, rows, ECELLS), jnp.float32),
+        out_shape=jax.ShapeDtypeStruct((devices, per_pair * 4 * rows + more_rows, LANES), jnp.float32),
         name="filter%d" % first_slot,
-    )(target, counts, start_vectors, conductance)
+    )(target, counts, source, start_vectors, conductance, *more)
 
 
 def pack(blocks):
@@ -191,8 +205,68 @@
     return tile[:, (k % 2) * vectors : (k % 2 + 1) * vectors]
 
 
-def packed_width(blocks):
-    return (blocks + 1) // 2 * LANES
+def hypercube_bits(block, size):
+    place, distance = 0, size // 2
+    while distance:
+        place += distance * (block & 1)
+        block >>= 1
+        distance //= 2
+    return place
+
+
+def hypercube_step(x, axis, size, distance):
+    there = lax.ppermute(x, axis, [(i, i ^ distance) for i in range(size)])
+    return jnp.concatenate([x, there], axis=0)
+
+
+def packed_rows(blocks):
+    return (blocks + 1) // 2 * ROWS
+
+
+def send_keys(elements, per_pair, source_ref, out_ref):
+    lane = lax.broadcasted_iota(jnp.int32, (ROWS, LANES), 1)
+
+    def place(d, carry):
+        tile = jnp.zeros((ROWS, LANES), jnp.int32)
+        for i in range(per_pair):
+            key = lax.rem(source_ref[d * per_pair + i], elements * 8)
+            tile = jnp.where(lane == i, key, tile)
+        out_ref[d] = tile.astype(jnp.float32)
+        return carry
+
+    lax.fori_loop(0, out_ref.shape[0], place, 0)
+
+
+def send_rows(per_pair, source_ref, in_ref, out_ref):
+    hoods, vectors, slots = in_ref.shape
+    fill = functools.partial(fill_rows, per_pair, source_ref, in_ref, out_ref)
+    pl.run_scoped(fill, pltpu.VMEM((hoods, slots, vectors), jnp.float32))
+
+
+def fill_rows(per_pair, source_ref, in_ref, out_ref, rows_ref):
+    groups = lax.axis_size("eight")
+    hoods, _, slots = in_ref.shape
+    owned = hoods // groups
+    width = slots // groups
+    bits = width // ROWS
+    me = lax.axis_index("eight")
+    for block in range(groups):
+        e = me ^ hypercube_bits(block, groups)
+        for n in range(owned):
+            rows_ref[e * owned + n] = jnp.transpose(in_ref[block * owned + n])
+
+    def place(d, carry):
+        blocks = []
+        for i in range(per_pair):
+            n = source_ref[d * per_pair + i]
+            for r in range(bits):
+                at = pl.multiple_of(me * width + r * ROWS, ROWS)
+                blocks.append(rows_ref[n, pl.ds(at, ROWS), :])
+        for k, tile in enumerate(pack(blocks)):
+            out_ref[d, k * ROWS : (k + 1) * ROWS, :] = tile
+        return carry
+
+    lax.fori_loop(0, out_ref.shape[0], place, 0)
 
 
 def sum_kernel(per_pair, source_ref, in_ref, after_ref, out_ref, rows_ref):
@@ -208,7 +282,7 @@
             n = source_ref[d * per_pair + i]
             for r in range(bits):
                 k = i * bits + r
-                rows_ref[n, r * ROWS : (r + 1) * ROWS, :] += half(in_ref[d, :, k // 2 * LANES : (k // 2 + 1) * LANES], k)
+                rows_ref[n, r * ROWS : (r + 1) * ROWS, :] += half(in_ref[d, k // 2 * ROWS : (k // 2 + 1) * ROWS, :], k)
         return carry
 
     lax.fori_loop(0, in_ref.shape[0], gather, 0)
@@ -217,7 +291,7 @@
             rows_ref[e * owned + n, r * ROWS : (r + 1) * ROWS, :] for n in range(owned) for r in range(bits)
         ]
         for i, tile in enumerate(pack(blocks)):
-            out_ref[e, :, i * LANES : (i + 1) * LANES] = tile
+            out_ref[e, i * ROWS : (i + 1) * ROWS, :] = tile
 
 
 def coarse_out_kernel(in_ref, out_ref):
@@ -229,7 +303,7 @@
         for e in range(groups):
             for r in range(bits):
                 k = n * bits + r
-                rows.append(half(in_ref[e, :, k // 2 * LANES : (k // 2 + 1) * LANES], k))
+                rows.append(half(in_ref[e, k // 2 * ROWS : (k // 2 + 1) * ROWS, :], k))
         out_ref[n] = jnp.transpose(jnp.concatenate(rows, axis=0))
 
 
@@ -248,48 +322,73 @@
 def start_gather(chunks, groups, per_pair, e, from_ref, got_refs, phi_ref, sems):
     width = sum(count for _, count in chunks) * ROWS
     for o in range(8):
-        base = from_ref[e * 8 + o]
+        source = from_ref[e * 8 + o]
+        device = lax.div(source, per_pair) * groups
+        i = lax.rem(source, per_pair)
         for g in range(groups):
-            q = base + g * per_pair
             row = (e * 8 + o) * groups * width + g * width
             for k, (first, count) in enumerate(chunks):
-                rows = count * ROWS
                 pltpu.make_async_copy(
-                    got_refs[k].at[pl.ds(pl.multiple_of(q * rows, ROWS), rows)],
-                    phi_ref.at[pl.ds(row + first, rows)],
+                    got_refs[k].at[device + g, pl.ds(i * 4, 4)],
+                    phi_ref.at[:, pl.ds(row + first, count * ROWS)],
                     sems.at[e],
                 ).start()
 
 
-def wait_gather(e, rows, got_refs, phi_ref, sems):
-    pltpu.make_async_copy(
-        got_refs[-1].at[pl.ds(0, rows)], phi_ref.at[pl.ds(pl.multiple_of(e * rows, ROWS), rows)], sems.at[e]
-    ).wait()
-
-
-def applied_kernel(chunks, groups, per_pair, from_ref, hood_ref, key_ref, all_ref, cap_ref, *refs):
+def wait_gather(e, rows, phi_ref, sems):
+    part = phi_ref.at[:, pl.ds(pl.multiple_of(e * rows, ROWS), rows)]
+    pltpu.make_async_copy(part, part, sems.at[e]).wait()
+
+
+def basis_of(e, rows, phi_ref):
+    at = pl.ds(pl.multiple_of(e * rows, ROWS), rows)
+    return jnp.concatenate([phi_ref[p, at, :] for p in range(4)], axis=1)
+
+
+def dot(x, y, x_dim, y_dim):
+    return lax.dot_general(x, y, (((x_dim,), (y_dim,)), ((), ())), preferred_element_type=jnp.float32)
+
+
+def applied_kernel(chunks, groups, per_pair, from_ref, key_ref, cap_ref, *refs):
     got_refs = refs[: len(chunks)]
-    out_ref, phi_ref, r_ref, applied_ref, sems, r_sems = refs[len(chunks) :]
+    out_ref, phi_ref, rows_ref, r_ref, applied_ref, sems, rows_sem = refs[len(chunks) :]
     width = sum(count for _, count in chunks) * ROWS
     bits = width // ROWS
     slots = groups * width
     rows = 8 * slots
     elements = cap_ref.shape[0]
+    wide = out_ref.shape[0] // groups
+    per_block = rows_ref.shape[2] // ROWS
+    coarse = pltpu.make_async_copy(got_refs[-1].at[:, pl.ds(per_pair * 4, rows_ref.shape[1])], rows_ref, rows_sem)
+    coarse.start()
     for e in range(elements):
-        for o in range(8):
-            k = e * 8 + o
-            pltpu.make_async_copy(all_ref.at[hood_ref[k]], r_ref.at[k], r_sems.at[e]).start()
         start_gather(chunks, groups, per_pair, e, from_ref, got_refs, phi_ref, sems)
+    coarse.wait()
+
+    def place(w, carry):
+        for i in range(per_pair):
+            key = key_ref[w * per_pair + i] * slots
+            for g in range(groups):
+                for r in range(bits):
+                    k = i * bits + r
+                    t = k // 2
+                    at = t % per_block * ROWS
+                    row = pl.multiple_of(key + (g * width + r * ROWS), ROWS)
+                    r_ref[pl.ds(row, ROWS), :] = half(rows_ref[w * groups + g, t // per_block, at : at + ROWS, :], k)
+        return carry
+
+    lax.fori_loop(0, wide, place, 0)
     for e in range(elements):
-        pltpu.make_async_copy(all_ref.at[pl.ds(0, 8)], r_ref.at[pl.ds(e * 8, 8)], r_sems.at[e]).wait()
-        wait_gather(e, rows, got_refs, phi_ref, sems)
-        phi = split(phi_ref[e * rows : (e + 1) * rows, :])
-        sums = jnp.zeros((r_ref.shape[1], ECELLS), jnp.float32)
-        for o in range(8):
-            r = split(r_ref[e * 8 + o, :, :slots])
-            sums = sums + product(r, [x[o * slots : (o + 1) * slots] for x in phi], ((1,), (0,)))
-        sums = sums * cap_ref[e : e + 1, :]
-        applied_ref[e * rows : (e + 1) * rows, :] = product(phi, split(sums), ((1,), (1,)))
+        r = jnp.concatenate(split(jnp.transpose(r_ref[e * rows : (e + 1) * rows, :])), axis=0)
+        vectors = r.shape[0] // 2
+        wait_gather(e, rows, phi_ref, sems)
+        high, low = split(basis_of(e, rows, phi_ref))
+        both = dot(r, high, 1, 0)
+        sums = both[:vectors] + (both[vectors:] + dot(r[:vectors], low, 1, 0))
+        sums = jnp.concatenate(split(sums * cap_ref[e : e + 1, :]), axis=0)
+        both = dot(high, sums, 1, 1)
+        applied = both[:, :vectors] + (both[:, vectors:] + dot(low, sums[:vectors], 1, 1))
+        applied_ref[e * rows : (e + 1) * rows, :] = applied
 
     def back(w, carry):
         keys = [key_ref[w * per_pair + i] * slots for i in range(per_pair)]
@@ -300,10 +399,10 @@
                     row = pl.multiple_of(keys[i] + (g * width + r * ROWS), ROWS)
                     blocks.append(applied_ref[pl.ds(row, ROWS), :])
             for i, tile in enumerate(pack(blocks)):
-                out_ref[w * groups + g, :, i * LANES : (i + 1) * LANES] = tile
+                out_ref[w * groups + g, i * ROWS : (i + 1) * ROWS, :] = tile
         return carry
 
-    lax.fori_loop(0, out_ref.shape[0] // groups, back, 0)
+    lax.fori_loop(0, wide, back, 0)
 
 
 def galerkin_kernel(chunks, groups, per_pair, from_ref, cap_ref, *refs):
@@ -318,38 +417,12 @@
         for i in range(cap_ref.shape[0]):
             start_gather(chunks, groups, per_pair, i, from_ref, got_refs, phi_ref, sems)
 
-    wait_gather(e, rows, got_refs, phi_ref, sems)
-    phi = phi_ref[pl.ds(pl.multiple_of(e * rows, ROWS), rows), :]
-    weighted = phi * cap_ref[pl.ds(e, 1), :]
-    out_ref[0] = product(split(weighted), split(phi), ((1,), (1,)))
+    wait_gather(e, rows, phi_ref, sems)
+    phi = basis_of(e, rows, phi_ref)
+    out_ref[0] = product(split(phi * cap_ref[pl.ds(e, 1), :]), split(phi), ((1,), (1,)))
 
 
 CHUNKS = ((0, 1), (8, 2))
-
-
-def exchange_steps(wide, groups):
-    steps = []
-    for axis, size in (("wide", wide), ("eight", groups)):
-        distance = size // 2
-        while distance:
-            steps.append((axis, size, distance))
-            distance //= 2
-    return steps
-
-
-def gather_all(x, steps):
-    for axis, size, distance in steps:
-        there = lax.ppermute(x, axis, [(i, i ^ distance) for i in range(size)])
-        x = jnp.concatenate([x, there], axis=0)
-    return x
-
-
-def block_of(steps, wide_at, eight_at):
-    at = {"wide": wide_at ^ lax.axis_index("wide"), "eight": eight_at ^ lax.axis_index("eight")}
-    block = 0
-    for k, (axis, _, distance) in enumerate(steps):
-        block = block + jnp.where(at[axis] & distance, 1 << k, 0)
-    return block
 
 
 def body(start_vectors, conductance, counts, element_of, capacity, coarse_in):
@@ -372,65 +445,59 @@
     earlier = (owner[:, None] == owner[None, :]) & (order[None, :] < order[:, None])
     target = owner * per_pair + jnp.sum(earlier.astype(ints), axis=1)
 
-    got = []
-    held = (coarse_in, element_of, capacity, target)
-    for at, count in chunks:
-        send = filter_call(at, count, target, counts, start_vectors, conductance)
-        held, send = lax.optimization_barrier((held, send))
-        send = send.reshape(devices, per_pair, count * ROWS, ECELLS)
+    hit = target[None, :] == order[:, None]
+    local = (element_of % elements * 8 + jnp.arange(8, dtype=ints)[None, :]).reshape(-1)
+    keys = jnp.sum(jnp.where(hit, local[None, :], 0), axis=1)
+    source = jnp.sum(jnp.where(hit, order[None, :] // 8, 0), axis=1)
+    far = packed_rows(per_pair * bits)
+    near = packed_rows(owned * bits)
+
+    def exchange(send, rows):
         arrived = lax.all_to_all(send, both, split_axis=0, concat_axis=0, tiled=True)
-        got.append(arrived.reshape(pieces * count * ROWS, ECELLS))
-    coarse_in, element_of, capacity, late_target = held
-
-    steps = exchange_steps(wide, groups)
-    own = lax.dynamic_slice_in_dim(element_of, lax.axis_index("eight") * owned, owned, axis=0)
-    margin = jnp.zeros((owned, vectors, LANES - slots), jnp.float32).at[:, 0, :8].set(own.astype(jnp.float32))
-    every = gather_all(jnp.concatenate([jnp.swapaxes(coarse_in, 1, 2), margin], axis=2), steps)
-
-    wide_at = jnp.arange(wide, dtype=ints)[:, None]
-    eight_at = jnp.arange(groups, dtype=ints)[None, :]
-    block = block_of(steps, wide_at, eight_at)
-    incidence = every[:, 0, slots : slots + 8].reshape(devices, owned * 8)[block.reshape(-1)]
-    incidence = incidence.astype(ints).reshape(wide, pieces)
-    me = lax.axis_index("wide") * groups + lax.axis_index("eight")
-    mine = incidence // elements == me
-    before = (order[:, None] < order[None, :]).astype(jnp.float32)
-    rank = jnp.dot(mine.astype(jnp.float32), before).astype(ints)
-    key = incidence % elements * 8 + order[None, :] % 8
-    hood = (block[:, :, None] * owned + jnp.arange(owned, dtype=ints)).reshape(wide, hoods)
-    hood = jnp.broadcast_to(hood[:, :, None], (wide, hoods, 8)).reshape(wide, pieces)
-    first = wide_at * (groups * per_pair) + rank
-    chosen = mine[None] & (key[None] == jnp.arange(elements * 8, dtype=ints)[:, None, None])
-    from_at = jnp.sum(jnp.where(chosen, first[None], 0), axis=(1, 2))
-    hood_at = jnp.sum(jnp.where(chosen, hood[None], 0), axis=(1, 2))
-    placed = mine[:, None, :] & (rank[:, None, :] == jnp.arange(per_pair, dtype=ints)[None, :, None])
-    key_at = jnp.sum(jnp.where(placed, key[:, None, :], 0), axis=2).reshape(-1)
-    hit = late_target[None, :] == order[:, None]
-    source = jnp.sum(jnp.where(hit, order[None, :] // 8, 0), axis=1)
-
-    near = packed_width(owned * bits)
-    far = packed_width(per_pair * bits)
+        return arrived.reshape(devices, -1, rows, LANES)
+
+    filtered = functools.partial(filter_call, devices=devices, target=target, counts=counts)
+    filtered = functools.partial(filtered, start_vectors=start_vectors, conductance=conductance)
+    distance = groups // 2
+    coarse = hypercube_step(jnp.swapaxes(coarse_in, 1, 2), "eight", groups, distance)
+    (at, count), (late, more) = chunks
+    send = filtered(at, count, source=keys, extra=functools.partial(send_keys, elements), more_rows=ROWS)
+    coarse, send = lax.optimization_barrier((coarse, send))
+    first = exchange(send, count * ROWS)
+    while distance > 1:
+        distance //= 2
+        coarse = hypercube_step(coarse, "eight", groups, distance)
+    send = filtered(late, more, source=source, extra=send_rows, more_rows=far, more=(coarse,))
+    second = exchange(send, more * ROWS)
+    got = [first, second]
+
+    key_at = first[:: groups, 4 * per_pair, 0, :per_pair].astype(ints).reshape(-1)
+    chosen = key_at[None, :] == jnp.arange(elements * 8, dtype=ints)[:, None]
+    from_at = jnp.sum(jnp.where(chosen, jnp.arange(wide * per_pair, dtype=ints)[None, :], 0), axis=1)
+
     cap = capacity.reshape(elements, 2, HALF // 2, HALF, HALF).transpose(0, 2, 3, 1, 4).reshape(elements, ECELLS) / ECELLS
     rows = 8 * slots
-    phi = [pltpu.VMEM((elements * rows, ECELLS), jnp.float32)]
+    phi = [pltpu.VMEM((4, elements * rows, LANES), jnp.float32)]
     sems = [pltpu.SemaphoreType.DMA((elements,))]
     back = pl.pallas_call(
         functools.partial(applied_kernel, chunks, groups, per_pair),
         grid_spec=pltpu.PrefetchScalarGridSpec(
-            num_scalar_prefetch=3,
+            num_scalar_prefetch=2,
             grid=(),
-            in_specs=[ANY, VMEM] + [ANY] * len(chunks),
+            in_specs=[VMEM] + [ANY] * len(chunks),
             out_specs=VMEM,
             scratch_shapes=phi
             + [
-                pltpu.VMEM((elements * 8, vectors, LANES), jnp.float32),
+                pltpu.VMEM((devices, far // (more * ROWS), more * ROWS, LANES), jnp.float32),
+                pltpu.VMEM((elements * rows, vectors), jnp.float32),
                 pltpu.VMEM((elements * rows, vectors), jnp.float32),
             ]
-            + sems * 2,
+            + sems
+            + [pltpu.SemaphoreType.DMA],
         ),
-        out_shape=jax.ShapeDtypeStruct((devices, ROWS, far), jnp.float32),
+        out_shape=jax.ShapeDtypeStruct((devices, far, LANES), jnp.float32),
         name="applied",
-    )(from_at, hood_at, key_at, every, cap, *got)
+    )(from_at, key_at, cap, *got)
     returned = lax.all_to_all(back, both, split_axis=0, concat_axis=0, tiled=True)
     galerkin = pl.pallas_call(
         functools.partial(galerkin_kernel, chunks, groups, per_pair),
@@ -453,7 +520,7 @@
             out_specs=VMEM,
             scratch_shapes=[pltpu.VMEM((hoods, width, vectors), jnp.float32)],
         ),
-        out_shape=jax.ShapeDtypeStruct((groups, ROWS, near), jnp.float32),
+        out_shape=jax.ShapeDtypeStruct((groups, near, LANES), jnp.float32),
         name="sum_octants",
     )(source, returned, galerkin)
     out = lax.all_to_all(out, "eight", split_axis=0, concat_axis=0, tiled=True)

time: 299 us -> 253 us (0.85)
  waiting for transfers between devices: 159 us -> 131 us
  local copies, waits for them, and re-layouts: 13.1 us -> 2.32 us
  starting transfers between devices: 23.1 us -> 18 us
    ppermute x5 -> x2, waiting for transfers between devices: 136 us -> 1.29 us  [hypercube_step(): there = lax.ppermute(x, axis, [(i, i ^ distance) for i in range(size)])]
    all_to_all x2, waiting for transfers between devices: 15.3 us -> 122 us  [exchange(): lax.all_to_all(send, both, split_axis=0, concat_axis=0, tiled=True)]
    unnamed x16 -> x12, local copies, waits for them, and re-layouts: 5.58 us -> 0.9 us
    pallas_call x2, Pallas kernels: 54.5 us -> 57.7 us  [filter_call(): pl.pallas_call(functools.partial(filter_kernel, first_slot, groups, per_p...]
    concatenate x2 -> x0, local copies, waits for them, and re-layouts: 3.02 us -> none  [gather_all(): x = jnp.concatenate([x, there], axis=0)]
  transfers between devices with their start and end apart: 8 -> 5, of which waited for: 7 -> 4; matrix products, arithmetic and copies ran while one was open for 5% -> 2% of each run, Pallas kernels for 15% -> 28%
where the time goes in v3:
time: 253 us
  waiting for transfers between devices  131 us (52%)
  Pallas kernels  88.6 us (35%)
  starting transfers between devices  18 us (7%)
  blocking collectives  8.27 us (3%)
  other arithmetic  3.12 us (1%)
    all_to_all x2, waiting for transfers between devices, exchange(): lax.all_to_all(send, both, split_axis=0, concat_axis=0, tiled=True)  122 us
    pallas_call x2, Pallas kernels, filter_call(): pl.pallas_call(functools.partial(filter_kernel, first_slot, groups, per_p...  57.7 us
    pallas_call x1, Pallas kernels, body(): pl.pallas_call(functools.partial(galerkin_kernel, chunks, groups, per_pai...  12.4 us
    pallas_call x1, Pallas kernels, body(): pl.pallas_call(functools.partial(applied_kernel, chunks, groups, per_pair...  11.6 us
    all_to_all x2, starting transfers between devices, exchange(): lax.all_to_all(send, both, split_axis=0, concat_axis=0, tiled=True)  9.18 us
    all_to_all x1, blocking collectives, body(): out = lax.all_to_all(out, 'eight', split_axis=0, concat_axis=0, tiled=True)  8.27 us
    all_to_all x1, waiting for transfers between devices, body(): lax.all_to_all(back, both, split_axis=0, concat_axis=0, tiled=True)  7.96 us
    all_to_all x1, starting transfers between devices, body(): lax.all_to_all(back, both, split_axis=0, concat_axis=0, tiled=True)  5.47 us
  transfers between devices with their start and end apart: 5, of which 4 were waited for; matrix products, arithmetic and copies ran while one was open for 2% of the time, Pallas kernels for 28%

profile of v3, /device:TPU:0, one launch (start us, length us, event | category | flops | bytes accessed | tf_op | source)
XLA Modules:
  0.0 252.5 jit_solution(15994024368460027378)
XLA Ops:
  0.6 3.1 %collective-permute-start = (f32[4,64,96]{2,1,0:T(8,128)}, f32[4,64,96]{2,1,0:T(8,128)S(1)}, u32[]{:S(2)}, u32[]{:S(2)}) collective-permute-start(f32[4,64,96]{2,1,0:T(8,128)} %bitcast.12), channel_id=1, source_target_pairs={{0,2},{1,3},{2,0},{3,1},{4,6},{5,7},{6,4},{7,5},{8,10},{9,11},{10,... | collective-permute-start | bytes 294920 | tf_op jit(solution)/shard_map/ppermute | solution.py:218
  3.7 0.7 fusion.2
  4.7 0.2 convert_reduce_fusion
  4.9 0.7 select_reduce_fusion
  5.6 21.4 %filter0.1 = f32[32,136,128]{2,1,0:T(8,128)} custom-call(s32[128]{0:T(128)} %copy-done.4, s32[16]{0:T(128)} %refs_1_.3, s32[128]{0:T(128)} %get-tuple-element.7.refs_2_, bf16[16,24,4096]{2,1,0:T(8,128)(2,1)} %refs_3_.3, f32[16,4096]{1,0:T(8,128)} %refs_4_.3), custom_call_target="tpu_custom_call" | custom-call | tf_op jit(solution)/shard_map/filter0/pallas_call | solution.py:172
  27.0 4.9 %all-to-all-start = ((f32[32,136,128]{2,1,0:T(8,128)}), f32[32,136,128]{2,1,0:T(8,128)S(1)}, u32[]{:S(2)}, u32[]{:S(2)}) async-start(f32[32,136,128]{2,1,0:T(8,128)} %filter0.1), calls=%async_computation | async-start | bytes 4456448 | tf_op jit(solution)/shard_map/all_to_all | solution.py:456
  31.9 0.3 collective-permute-start.1
  32.3 1.3 collective-permute-done.1
  33.5 0.9 pad_maximum_fusion.refs_5_
  34.4 36.3 %filter8.1 = f32[32,304,128]{2,1,0:T(8,128)} custom-call(s32[128]{0:T(128)} %copy-done.4, s32[16]{0:T(128)} %refs_1_.3, s32[128]{0:T(128)} %get-tuple-element.6.refs_2_.source_ref, bf16[16,24,4096]{2,1,0:T(8,128)(2,1)} %refs_3_.3, f32[16,4096]{1,0:T(8,128)} %refs_4_.3, f32[16,64,96]{2,1,0:T(8,128)} %pad_maximum_fusion.refs_5_), custom_call_target="tpu_custom_call" | custom-call | tf_op jit(solution)/shard_map/filter8/pallas_call | solution.py:172
  70.7 12.8 %all-to-all-done = f32[32,136,128]{2,1,0:T(8,128)S(1)} async-done(((f32[32,136,128]{2,1,0:T(8,128)}), f32[32,136,128]{2,1,0:T(8,128)S(1)}, u32[]{:S(2)}, u32[]{:S(2)}) %all-to-all-start) | async-done | bytes 2228256 | tf_op jit(solution)/shard_map/all_to_all | solution.py:456
  83.5 4.3 %all-to-all-start.1 = ((f32[32,304,128]{2,1,0:T(8,128)}), f32[32,304,128]{2,1,0:T(8,128)}, u32[]{:S(2)}, u32[]{:S(2)}) async-start(f32[32,304,128]{2,1,0:T(8,128)} %filter8.1), calls=%async_computation.1 | async-start | bytes 9961472 | tf_op jit(solution)/shard_map/all_to_all | solution.py:456
  87.9 0.1 copy.18
  88.0 0.8 div.40.cap_ref
  88.9 0.7 select_reduce_fusion.2.from_ref
  89.6 109.4 %all-to-all-done.1 = f32[32,304,128]{2,1,0:T(8,128)} async-done(((f32[32,304,128]{2,1,0:T(8,128)}), f32[32,304,128]{2,1,0:T(8,128)}, u32[]{:S(2)}, u32[]{:S(2)}) %all-to-all-start.1) | async-done | bytes 4980768 | tf_op jit(solution)/shard_map/all_to_all | solution.py:456
  199.0 11.6 %applied.1 = f32[32,48,128]{2,1,0:T(8,128)} custom-call(s32[32]{0:T(128)} %select_reduce_fusion.2.from_ref, s32[32]{0:T(128)} %copy-done.5, f32[4,512]{1,0:T(4,128)} %div.40.cap_ref, f32[32,17,8,128]{3,2,1,0:T(8,128)} %bitcast.8, f32[32,19,16,128]{3,2,1,0:T(8,128)} %bitcast.3.refs_1_), custom_call_target="tpu_custom_call" | custom-call | tf_op jit(solution)/shard_map/applied/pallas_call | solution.py:482
  210.6 5.5 %all-to-all-start.2 = ((f32[32,48,128]{2,1,0:T(8,128)}), f32[32,48,128]{2,1,0:T(8,128)S(1)}, u32[]{:S(2)}, u32[]{:S(2)}) async-start(f32[32,48,128]{2,1,0:T(8,128)} %applied.1), calls=%async_computation.2 | async-start | bytes 1572864 | tf_op jit(solution)/shard_map/all_to_all | solution.py:501
  216.1 12.4 %galerkin.1.after_ref = f32[4,768,768]{2,1,0:T(8,128)} custom-call(s32[32]{0:T(128)} %select_reduce_fusion.2.from_ref, f32[4,512]{1,0:T(4,128)} %div.40.cap_ref, f32[32,17,8,128]{3,2,1,0:T(8,128)} %bitcast.9, f32[32,19,16,128]{3,2,1,0:T(8,128)} %bitcast.3.refs_1_), custom_call_target="tpu_custom_call" | custom-call | tf_op jit(solution)/shard_map/galerkin/pallas_call | solution.py:502
  228.5 8.0 %all-to-all-done.2.in_ref = f32[32,48,128]{2,1,0:T(8,128)S(1)} async-done(((f32[32,48,128]{2,1,0:T(8,128)}), f32[32,48,128]{2,1,0:T(8,128)S(1)}, u32[]{:S(2)}, u32[]{:S(2)}) %all-to-all-start.2) | async-done | bytes 786464 | tf_op jit(solution)/shard_map/all_to_all | solution.py:501
  236.5 0.9 copy-done.1
  237.4 5.1 %sum_octants.1 = f32[4,48,128]{2,1,0:T(8,128)} custom-call(s32[128]{0:T(128)} %get-tuple-element.6.refs_2_.source_ref, f32[32,48,128]{2,1,0:T(8,128)} %copy-done.1, f32[4,768,768]{2,1,0:T(8,128)} %galerkin.1.after_ref), custom_call_target="tpu_custom_call" | custom-call | tf_op jit(solution)/shard_map/sum_octants/pallas_call | solution.py:514
  242.5 8.3 %all_to_all.20.in_ref = f32[4,48,128]{2,1,0:T(8,128)} all-to-all(f32[4,48,128]{2,1,0:T(8,128)} %sum_octants.1), channel_id=1, replica_groups=mesh['wide'=8,'eight'=4] {'eight'}, dimensions={0} | all-to-all | bytes 196608 | tf_op jit(solution)/shard_map/all_to_all | solution.py:526
  250.8 1.8 coarse_out.1
  (23 shorter events, 0.6 us)
Async XLA Ops:
  0.6 26.4 %copy-start.2 = (f32[4,96,64]{1,2,0:T(8,128)S(1)}, f32[4,96,64]{1,2,0:T(8,128)}, u32[]{:S(2)}) copy-start(f32[4,96,64]{1,2,0:T(8,128)} %param.11) | copy-start | bytes 294916
  0.6 26.4 %collective-permute-start = (f32[4,64,96]{2,1,0:T(8,128)}, f32[4,64,96]{2,1,0:T(8,128)S(1)}, u32[]{:S(2)}, u32[]{:S(2)}) collective-permute-start(f32[4,64,96]{2,1,0:T(8,128)} %bitcast.12), channel_id=1, source_target_pairs={{0,2},{1,3},{2,0},{3,1},{4,6},{5,7},{6,4},{7,5},{8,10},{9,11},{10,... | collective-permute-start | bytes 294920 | tf_op jit(solution)/shard_map/ppermute | solution.py:218
  4.9 0.7 copy-start.4
  27.0 56.4 %all-to-all-start = ((f32[32,136,128]{2,1,0:T(8,128)}), f32[32,136,128]{2,1,0:T(8,128)S(1)}, u32[]{:S(2)}, u32[]{:S(2)}) async-start(f32[32,136,128]{2,1,0:T(8,128)} %filter0.1), calls=%async_computation | async-start | bytes 4456448 | tf_op jit(solution)/shard_map/all_to_all | solution.py:456
  31.9 1.6 collective-permute-start.1
  70.7 17.1 %copy-start.3 = (f32[4,512]{1,0:T(4,128)S(1)}, f32[4,512]{1,0:T(4,128)}, u32[]{:S(2)}) copy-start(f32[4,512]{1,0:T(4,128)} %param.10) | copy-start | bytes 24580
  83.5 5.3 %copy-start = (f32[32,136,128]{2,1,0:T(8,128)}, f32[32,136,128]{2,1,0:T(8,128)S(1)}, u32[]{:S(2)}) copy-start(f32[32,136,128]{2,1,0:T(8,128)S(1)} %all-to-all-done) | copy-start | bytes 6684676
  83.5 115.5 %all-to-all-start.1 = ((f32[32,304,128]{2,1,0:T(8,128)}), f32[32,304,128]{2,1,0:T(8,128)}, u32[]{:S(2)}, u32[]{:S(2)}) async-start(f32[32,304,128]{2,1,0:T(8,128)} %filter8.1), calls=%async_computation.1 | async-start | bytes 9961472 | tf_op jit(solution)/shard_map/all_to_all | solution.py:456
  88.9 110.1 %copy-start.5 = (s32[32]{0:T(128)}, s32[32]{0:T(128)S(1)}, u32[]{:S(2)}) copy-start(s32[32]{0:T(128)S(1)} %convert_element_type.16.key_ref) | copy-start | bytes 388
  210.6 25.9 %all-to-all-start.2 = ((f32[32,48,128]{2,1,0:T(8,128)}), f32[32,48,128]{2,1,0:T(8,128)S(1)}, u32[]{:S(2)}, u32[]{:S(2)}) async-start(f32[32,48,128]{2,1,0:T(8,128)} %applied.1), calls=%async_computation.2 | async-start | bytes 1572864 | tf_op jit(solution)/shard_map/all_to_all | solution.py:501
  236.5 0.9 copy-start.1

commit v4 on v3

v4 whole, which is shorter than its diff:
```python
import functools

import jax
import jax.numpy as jnp
from jax import lax
from jax.experimental import pallas as pl
from jax.experimental.pallas import tpu as pltpu
from jax.sharding import PartitionSpec as P

SIDE = 16
PASSES = 6
ECELLS = 512
LANES = 128
ROWS = 8
HALF = SIDE // 2
TILES = SIDE * SIDE * SIDE // LANES
PAIR = SIDE * SIDE // LANES

ANY = pl.BlockSpec(memory_space=pltpu.HBM)
VMEM = pl.BlockSpec(memory_space=pltpu.VMEM)
SCOPED = pltpu.CompilerParams(vmem_limit_bytes=28 << 20)


def hat(i):
    return min(i + 0.5, SIDE - 0.5 - i) / HALF


def stencil_table(cond, w_ref):
    cells = cond.shape[1]
    at = lax.broadcasted_iota(jnp.int32, cond.shape, 1)
    diagonal = jnp.zeros_like(cond)
    links = []
    for stride in (SIDE * SIDE, SIDE, 1):
        position = (at // stride) % SIDE
        for toward in (-1, 1):
            beside = pltpu.roll(cond, (-toward * stride) % cells, 1)
            inside = (position + toward >= 0) & (position + toward < SIDE)
            face = 0.5 * (cond + jnp.where(inside, beside, cond))
            diagonal = diagonal + face
            links.append(jnp.where(inside, face, 0.0))
    upper = 2.0 * jnp.max(diagonal, axis=1, keepdims=True)
    twice = 2.0 / (0.4375 * upper)
    table = [(diagonal - 0.5625 * upper) * twice] + [link * twice for link in links]
    for i, values in enumerate(table):
        for t in range(TILES):
            w_ref[i, t] = values[:, t * LANES : (t + 1) * LANES]


def filter_kernel(first_slot, groups, per_pair, elements, extra, *refs):
    element_ref, counts_ref, sv_ref, cond_ref = refs[:4]
    extra_refs, refs = refs[4:-9], refs[-9:]
    send_ref, w_ref, y_ref, out_ref, sems, more_ref, more_sem, used_ref, note_ref = refs
    n = pl.program_id(0)
    devices = send_ref.shape[0]

    last = pl.num_programs(0) - 1
    rows = groups * ROWS
    lane = lax.broadcasted_iota(jnp.int32, (ROWS, LANES), 1)
    low_row = lane < SIDE
    high_row = lane >= LANES - SIDE

    @pl.when(n == 0)
    def _():
        stencil_table(cond_ref[...], w_ref)
        for d in range(devices):
            used_ref[d] = 0

    targets = []
    for o in range(8):
        element = element_ref[n, o]
        owner = lax.div(element, elements)
        i = used_ref[owner]
        used_ref[owner] = i + 1
        note_ref[owner * per_pair + i] = (n * elements + lax.rem(element, elements)) * 8 + o
        targets.append((owner, i))

    def weight(k, t):
        return w_ref[k, t, pl.ds(n, ROWS, 0), :]

    start = sv_ref[0].astype(jnp.float32)
    for g in range(groups):
        y_ref[0, g] = start[first_slot + g * ROWS : first_slot + (g + 1) * ROWS, :]

    squares = [jnp.zeros((ROWS, LANES), jnp.float32) for _ in range(groups)]
    for sweep in range(PASSES):
        src, dst, old = sweep % 3, (sweep + 1) % 3, (sweep + 2) % 3

        def tile(g, a, d):
            t = a * PAIR + d
            return y_ref[src, g, :, t * LANES : (t + 1) * LANES]

        window = [[None] + [[tile(g, a, d) for d in range(PAIR)] for a in range(1)] for g in range(groups)]
        for a in range(SIDE):
            ups = []
            for g in range(groups):
                below, here = window[g]
                above = [tile(g, a + 1, d) for d in range(PAIR)] if a + 1 < SIDE else None
                ups.append((below, here, above))
                window[g] = [here, above]
            back = [[pltpu.roll(u[1][d], SIDE, 1) for d in range(PAIR)] for u in ups]
            fore = [[pltpu.roll(u[1][d], LANES - SIDE, 1) for d in range(PAIR)] for u in ups]
            for d in range(PAIR):
                t = a * PAIR + d
                w = [weight(k, t) for k in range(7)]
                for g in range(groups):
                    below, here, above = ups[g]
                    value = w[0] * here[d]
                    if below is not None:
                        value = value - w[1] * below[d]
                    if above is not None:
                        value = value - w[2] * above[d]
                    lower = back[g][d] if d == 0 else jnp.where(low_row, back[g][d - 1], back[g][d])
                    upper = fore[g][d] if d == PAIR - 1 else jnp.where(high_row, fore[g][d + 1], fore[g][d])
                    value = value - w[3] * lower
                    value = value - w[4] * upper
                    value = value - w[5] * pltpu.roll(here[d], 1, 1)
                    value = value - w[6] * pltpu.roll(here[d], LANES - 1, 1)
                    if sweep == 0:
                        value = 0.5 * value
                    else:
                        value = value - y_ref[old, g, :, t * LANES : (t + 1) * LANES]
                    y_ref[dst, g, :, t * LANES : (t + 1) * LANES] = value
                    if sweep == PASSES - 1:
                        squares[g] = squares[g] + value * value
    final = PASSES % 3

    slot = lax.rem(n, 2)

    def copy_out(step_slot, target, o):
        at = pl.multiple_of(target[1] * (4 * rows), ROWS)
        place = send_ref.at[target[0], pl.ds(at, 4 * rows)]
        return pltpu.make_async_copy(out_ref.at[step_slot, o], place, sems.at[step_slot, o])

    @pl.when(n >= 2)
    def _():
        for o in range(8):
            copy_out(slot, (0, 0), o).wait()

    column = lax.rem(lax.div(lane, SIDE), HALF)
    across = (lax.rem(lane, SIDE)).astype(jnp.float32)
    hat_c = jnp.minimum(across + 0.5, SIDE - 0.5 - across) / HALF
    even = lax.rem(lax.div(lane, HALF), 2) == 0
    bumps = []
    for d in range(PAIR):
        along = (column + d * HALF).astype(jnp.float32)
        bumps.append(hat_c * (jnp.minimum(along + 0.5, SIDE - 0.5 - along) / HALF))
    base = lax.axis_index("eight") * sv_ref.shape[1] + first_slot
    for g in range(groups):
        mean = jnp.sum(squares[g], axis=1, keepdims=True) / (TILES * LANES)
        row = lax.broadcasted_iota(jnp.int32, (ROWS, 1), 0) + (base + g * ROWS)
        scale = lax.rsqrt(mean + 1e-05) * (row < counts_ref[n]).astype(jnp.float32)
        for d in range(PAIR):
            weight_d = scale * bumps[d]
            for dx in range(2):
                for p in range(HALF // 2):
                    pair = []
                    for h in range(2):
                        a = dx * HALF + h * (HALF // 2) + p
                        t = a * PAIR + d
                        pair.append(y_ref[final, g, :, t * LANES : (t + 1) * LANES] * (weight_d * hat(a)))
                    near = jnp.where(even, pair[0], pltpu.roll(pair[1], HALF, 1))
                    far = jnp.where(even, pltpu.roll(pair[0], LANES - HALF, 1), pair[1])
                    for dz, value in enumerate((near, far)):
                        at = p * rows + g * ROWS
                        out_ref[slot, dx * 4 + d * 2 + dz, at : at + ROWS, :] = value
    for o in range(8):
        copy_out(slot, targets[o], o).start()

    @pl.when(n == last)
    def _():
        extra(per_pair, elements, note_ref, *extra_refs, more_ref)
        base = per_pair * 4 * rows
        more = pltpu.make_async_copy(more_ref, send_ref.at[:, pl.ds(base, more_ref.shape[1])], more_sem)
        more.start()
        more.wait()
        for o in range(8):
            copy_out(1 - slot, (0, 0), o).wait()
        for o in range(8):
            copy_out(slot, (0, 0), o).wait()


def filter_call(first_slot, groups, devices, elements, element_of, counts, start_vectors, conductance, extra, more_rows, more=()):
    hoods, width, cells = start_vectors.shape
    rows = groups * ROWS
    per_pair = hoods * 8 // devices
    return pl.pallas_call(
        functools.partial(filter_kernel, first_slot, groups, per_pair, elements, extra),
        grid_spec=pltpu.PrefetchScalarGridSpec(
            num_scalar_prefetch=2,
            grid=(hoods,),
            in_specs=[
                pl.BlockSpec((1, width, cells), lambda n, *_: (n, 0, 0)),
                pl.BlockSpec((hoods, cells), lambda n, *_: (0, 0)),
            ]
            + [pl.BlockSpec(x.shape, lambda n, *_, k=x.ndim: (0,) * k) for x in more],
            out_specs=ANY,
            scratch_shapes=[
                pltpu.VMEM((7, TILES, hoods, LANES), jnp.float32),
                pltpu.VMEM((3, groups, ROWS, cells), jnp.float32),
                pltpu.VMEM((2, 8, 4 * rows, LANES), jnp.float32),
                pltpu.SemaphoreType.DMA((2, 8)),
                pltpu.VMEM((devices, more_rows, LANES), jnp.float32),
                pltpu.SemaphoreType.DMA,
                pltpu.SMEM((devices,), jnp.int32),
                pltpu.SMEM((hoods * 8,), jnp.int32),
            ],
        ),
        out_shape=pltpu.HBM((devices, per_pair * 4 * rows + more_rows, LANES), jnp.float32),
        compiler_params=SCOPED,
        name="filter%d" % first_slot,
    )(element_of, counts, start_vectors, conductance, *more)


def pack(pieces):
    if len(pieces) % 2:
        pieces = pieces + [[jnp.zeros_like(x) for x in pieces[0]]]
    return [
        jnp.concatenate(pair, axis=1) for i in range(0, len(pieces), 2) for pair in zip(pieces[i], pieces[i + 1])
    ]


def part(i, r, bits):
    t = (i // 2 * bits + r) * ROWS
    return slice(t, t + ROWS), slice(i % 2 * (LANES // 2), (i % 2 + 1) * (LANES // 2))


def hypercube_bits(block, size):
    place, distance = 0, size // 2
    while distance:
        place += distance * (block & 1)
        block >>= 1
        distance //= 2
    return place


def hypercube_step(x, axis, size, distance):
    there = lax.ppermute(x, axis, [(i, i ^ distance) for i in range(size)])
    return jnp.concatenate([x, there], axis=0)


def packed_rows(pieces, bits):
    return (pieces + 1) // 2 * bits * ROWS


def send_keys(per_pair, elements, note_ref, out_ref):
    lane = lax.broadcasted_iota(jnp.int32, (ROWS, LANES), 1)

    def place(d, carry):
        tile = jnp.zeros((ROWS, LANES), jnp.int32)
        for i in range(per_pair):
            tile = jnp.where(lane == i, lax.rem(note_ref[d * per_pair + i], elements * 8), tile)
        out_ref[d] = tile.astype(jnp.float32)
        return carry

    lax.fori_loop(0, out_ref.shape[0], place, 0)


def send_rows(per_pair, elements, note_ref, in_ref, out_ref):
    hoods, vectors, slots = in_ref.shape
    fill = functools.partial(fill_rows, per_pair, elements, note_ref, in_ref, out_ref)
    pl.run_scoped(fill, pltpu.VMEM((hoods, slots, vectors), jnp.float32))


def fill_rows(per_pair, elements, note_ref, in_ref, out_ref, rows_ref):
    groups = lax.axis_size("eight")
    hoods, _, slots = in_ref.shape
    owned = hoods // groups
    width = slots // groups
    me = lax.axis_index("eight")
    for block in range(groups):
        e = me ^ hypercube_bits(block, groups)
        for n in range(owned):
            rows_ref[e * owned + n] = jnp.transpose(in_ref[block * owned + n])

    def place(d, carry):
        pieces = []
        for i in range(per_pair):
            n = lax.div(note_ref[d * per_pair + i], elements * 8)
            at = [pl.multiple_of(me * width + r, ROWS) for r in range(0, width, ROWS)]
            pieces.append([rows_ref[n, pl.ds(x, ROWS), :] for x in at])
        for k, tile in enumerate(pack(pieces)):
            out_ref[d, k * ROWS : (k + 1) * ROWS, :] = tile
        return carry

    lax.fori_loop(0, out_ref.shape[0], place, 0)


def sum_kernel(per_pair, bits, target_ref, in_ref, after_ref, *out_refs):
    del after_ref
    groups = len(out_refs)
    owned = target_ref.shape[0] // 8 // groups
    me = lax.axis_index("eight")
    left = lax.broadcasted_iota(jnp.int32, (ROWS, LANES), 1) < LANES // 2
    for distance, out_ref in enumerate(out_refs):
        pieces = []
        for k in range(owned):
            n = (me ^ distance) * owned + k
            sums = [jnp.zeros((ROWS, LANES), jnp.float32)] * bits
            for o in range(8):
                target = target_ref[n * 8 + o]
                i = lax.rem(target, per_pair)
                first = lax.div(i, 2) * bits
                wanted = left == (lax.rem(i, 2) == 0)
                for r in range(bits):
                    at = pl.multiple_of((first + r) * ROWS, ROWS)
                    sums[r] += jnp.where(wanted, in_ref[lax.div(target, per_pair), pl.ds(at, ROWS), :], 0.0)
            pieces.append([x[:, : LANES // 2] + x[:, LANES // 2 :] for x in sums])
        for i, tile in enumerate(pack(pieces)):
            out_ref[i * ROWS : (i + 1) * ROWS, :] = tile


def coarse_out_kernel(bits, *refs):
    in_refs, out_ref, rows_ref = refs[:-2], refs[-2], refs[-1]
    me = lax.axis_index("eight")
    for distance, in_ref in enumerate(in_refs):
        for n in range(out_ref.shape[0]):
            for r in range(bits):
                at = pl.multiple_of((me ^ distance) * (bits * ROWS) + r * ROWS, ROWS)
                rows, lanes = part(n, r, bits)
                rows_ref[n, pl.ds(at, ROWS), :] = in_ref[rows, lanes]
    for n in range(out_ref.shape[0]):
        out_ref[n] = jnp.transpose(rows_ref[n])


def split(x):
    high = x.astype(jnp.bfloat16)
    return high, (x - high.astype(jnp.float32)).astype(jnp.bfloat16)


def product(x, y, dims):
    xh, xl = x
    yh, yl = y
    dot = functools.partial(lax.dot_general, dimension_numbers=(dims, ((), ())), preferred_element_type=jnp.float32)
    return dot(xh, yh) + (dot(xh, yl) + dot(xl, yh))


def basis_of(e, chunks, groups, per_pair, from_ref, got_refs):
    columns = [[] for _ in range(4)]
    for o in range(8):
        source = from_ref[e * 8 + o]
        device = lax.div(source, per_pair) * groups
        i = lax.rem(source, per_pair)
        for g in range(groups):
            for k, (_, count) in enumerate(chunks):
                rows = count * ROWS
                for p in range(4):
                    at = pl.multiple_of(i * (4 * rows) + p * rows, ROWS)
                    columns[p].append(got_refs[k][device + g, pl.ds(at, rows), :])
    return jnp.concatenate([jnp.concatenate(x, axis=0) for x in columns], axis=1)


def dot(x, y, x_dim, y_dim):
    return lax.dot_general(x, y, (((x_dim,), (y_dim,)), ((), ())), preferred_element_type=jnp.float32)


def applied_kernel(chunks, groups, per_pair, from_ref, key_ref, cap_ref, *refs):
    got_refs = refs[: len(chunks)]
    out_ref, r_ref, applied_ref = refs[len(chunks) :]
    width = sum(count for _, count in chunks) * ROWS
    bits = width // ROWS
    slots = groups * width
    rows = 8 * slots
    elements = cap_ref.shape[0]
    wide = out_ref.shape[0] // groups
    base = per_pair * 4 * chunks[-1][1] * ROWS

    def place(w, carry):
        for i in range(per_pair):
            key = key_ref[w * per_pair + i] * slots
            for g in range(groups):
                for r in range(bits):
                    at, lanes = part(i, r, bits)
                    row = pl.multiple_of(key + (g * width + r * ROWS), ROWS)
                    r_ref[pl.ds(row, ROWS), :] = got_refs[-1][w * groups + g, base + at.start : base + at.stop, lanes]
        return carry

    lax.fori_loop(0, wide, place, 0)
    for e in range(elements):
        r = jnp.concatenate(split(jnp.transpose(r_ref[e * rows : (e + 1) * rows, :])), axis=0)
        vectors = r.shape[0] // 2
        high, low = split(basis_of(e, chunks, groups, per_pair, from_ref, got_refs))
        both = dot(r, high, 1, 0)
        sums = both[:vectors] + (both[vectors:] + dot(r[:vectors], low, 1, 0))
        sums = jnp.concatenate(split(sums * cap_ref[e : e + 1, :]), axis=0)
        both = dot(high, sums, 1, 1)
        applied = both[:, :vectors] + (both[:, vectors:] + dot(low, sums[:vectors], 1, 1))
        applied_ref[e * rows : (e + 1) * rows, :] = applied

    def back(w, carry):
        keys = [key_ref[w * per_pair + i] * slots for i in range(per_pair)]
        for g in range(groups):
            at = [g * width + r for r in range(0, width, ROWS)]
            pieces = [[applied_ref[pl.ds(pl.multiple_of(key + x, ROWS), ROWS), :] for x in at] for key in keys]
            for i, tile in enumerate(pack(pieces)):
                out_ref[w * groups + g, i * ROWS : (i + 1) * ROWS, :] = tile
        return carry

    lax.fori_loop(0, wide, back, 0)


def galerkin_kernel(chunks, groups, per_pair, from_ref, cap_ref, *refs):
    got_refs, out_ref = refs[:-1], refs[-1]
    e = pl.program_id(0)
    phi = basis_of(e, chunks, groups, per_pair, from_ref, got_refs)
    out_ref[0] = product(split(phi * cap_ref[pl.ds(e, 1), :]), split(phi), ((1,), (1,)))


CHUNKS = ((0, 1), (8, 2))


def body(start_vectors, conductance, counts, element_of, capacity, coarse_in):
    groups = lax.axis_size("eight")
    wide = lax.axis_size("wide")
    devices = wide * groups
    hoods, width, cells = start_vectors.shape
    owned = hoods // groups
    elements = capacity.shape[0]
    pieces = hoods * 8
    per_pair = pieces // devices
    slots, vectors = coarse_in.shape[1:]
    bits = width // ROWS
    chunks = CHUNKS
    both = ("wide", "eight")
    ints = jnp.int32

    far = packed_rows(per_pair, bits)
    in_vmem = functools.partial(pltpu.with_memory_space_constraint, memory_space=pltpu.VMEM)
    in_hbm = functools.partial(pltpu.with_memory_space_constraint, memory_space=pltpu.HBM)

    def exchange(send):
        return lax.all_to_all(send, both, split_axis=0, concat_axis=0, tiled=True)

    filtered = functools.partial(filter_call, devices=devices, elements=elements, element_of=element_of)
    filtered = functools.partial(filtered, counts=counts, start_vectors=in_hbm(start_vectors), conductance=in_hbm(conductance))
    distance = groups // 2
    coarse = hypercube_step(jnp.swapaxes(coarse_in, 1, 2), "eight", groups, distance)
    (at, count), (late, more) = chunks
    send = filtered(at, count, extra=send_keys, more_rows=ROWS)
    coarse, later_element_of, capacity, send = lax.optimization_barrier((coarse, element_of, capacity, send))
    first = exchange(send)
    while distance > 1:
        distance //= 2
        coarse = hypercube_step(coarse, "eight", groups, distance)
    send = filtered(late, more, extra=send_rows, more_rows=far, more=(coarse,))
    second = exchange(send)
    got = [in_vmem(first), in_vmem(second)]

    owner = (later_element_of // elements).reshape(-1)
    order = jnp.arange(pieces, dtype=ints)
    earlier = (owner[:, None] == owner[None, :]) & (order[None, :] < order[:, None])
    target = owner * per_pair + jnp.sum(earlier.astype(ints), axis=1)
    key_at = first[::groups, 4 * per_pair * count * ROWS, :per_pair].astype(ints).reshape(-1)
    chosen = key_at[None, :] == jnp.arange(elements * 8, dtype=ints)[:, None]
    from_at = jnp.sum(jnp.where(chosen, jnp.arange(wide * per_pair, dtype=ints)[None, :], 0), axis=1)

    cap = capacity.reshape(elements, 2, HALF // 2, HALF, HALF).transpose(0, 2, 3, 1, 4).reshape(elements, ECELLS) / ECELLS
    rows = 8 * slots
    back = pl.pallas_call(
        functools.partial(applied_kernel, chunks, groups, per_pair),
        grid_spec=pltpu.PrefetchScalarGridSpec(
            num_scalar_prefetch=2,
            grid=(),
            in_specs=[VMEM] * (1 + len(chunks)),
            out_specs=VMEM,
            scratch_shapes=[pltpu.VMEM((elements * rows, vectors), jnp.float32)] * 2,
        ),
        out_shape=pltpu.HBM((devices, far, LANES), jnp.float32),
        compiler_params=SCOPED,
        name="applied",
    )(from_at, key_at, cap, *got)
    returned = in_vmem(exchange(back))
    galerkin = pl.pallas_call(
        functools.partial(galerkin_kernel, chunks, groups, per_pair),
        grid_spec=pltpu.PrefetchScalarGridSpec(
            num_scalar_prefetch=1,
            grid=(elements,),
            in_specs=[pl.BlockSpec((elements, ECELLS), lambda e, i: (0, 0))] + [VMEM] * len(chunks),
            out_specs=pl.BlockSpec((1, rows, rows), lambda e, i: (e, 0, 0)),
        ),
        out_shape=pltpu.HBM((elements, rows, rows), jnp.float32),
        compiler_params=SCOPED,
        name="galerkin",
    )(from_at, cap, *got)
    near = packed_rows(owned, bits)
    outs = pl.pallas_call(
        functools.partial(sum_kernel, per_pair, bits),
        grid_spec=pltpu.PrefetchScalarGridSpec(
            num_scalar_prefetch=1,
            grid=(),
            in_specs=[VMEM, ANY],
            out_specs=[VMEM] * groups,
        ),
        out_shape=[jax.ShapeDtypeStruct((near, LANES), jnp.float32)] * groups,
        compiler_params=SCOPED,
        name="sum_octants",
    )(target, returned, in_hbm(galerkin))
    ends = [outs[0]]
    for distance in range(1, groups):
        ends.append(in_vmem(lax.ppermute(outs[distance], "eight", [(i, i ^ distance) for i in range(groups)])))
    coarse_out = pl.pallas_call(
        functools.partial(coarse_out_kernel, bits),
        in_specs=[VMEM] * groups,
        out_specs=VMEM,
        out_shape=jax.ShapeDtypeStruct((owned, vectors, slots), jnp.float32),
        scratch_shapes=[pltpu.VMEM((owned, slots, vectors), jnp.float32)],
        compiler_params=SCOPED,
        name="coarse_out",
    )(*ends)
    return (galerkin, jnp.swapaxes(coarse_out, 1, 2))


def solution(mesh):
    in_specs = (
        P("wide", "eight", None),
        P("wide", None),
        P("wide"),
        P("wide", None),
        P(("wide", "eight"), None),
        P(("wide", "eight"), None, None),
    )
    out_specs = (P(("wide", "eight"), None, None), P(("wide", "eight"), None, None))
    return jax.shard_map(body, mesh=mesh, in_specs=in_specs, out_specs=out_specs, check_vma=False)
```

time: 253 us -> 241 us (0.953)
  blocking collectives: 8.27 us -> 0 us
  Pallas kernels: 88.6 us -> 81.5 us
  waiting for transfers between devices: 131 us -> 136 us
  other arithmetic: 3.12 us -> 0.39 us
    all_to_all x1 -> x0, blocking collectives: 8.27 us -> none  [body(): out = lax.all_to_all(out, 'eight', split_axis=0, concat_axis=0, tiled=True)]
    pallas_call x2, Pallas kernels: 6.92 us -> 2.41 us  [the longest x1 1.55 us: body(): pl.pallas_call(functools.partial(sum_kernel, per_pair, bits), grid_spec=p...]
    ppermute x0 -> x3, waiting for transfers between devices: none -> 3.14 us  [body(): lax.ppermute(outs[distance], 'eight', [(i, i ^ distance) for i in range(g...]
    pallas_call x1, Pallas kernels: 11.6 us -> 8.79 us  [body(): pl.pallas_call(functools.partial(applied_kernel, chunks, groups, per_pair...]
  transfers between devices with their start and end apart: 5 -> 8, of which waited for: 4 -> 6; matrix products, arithmetic and copies ran while one was open for 2% -> 1% of each run, Pallas kernels for 28% -> 29%
where the time goes in v4:
time: 241 us
  waiting for transfers between devices  136 us (56%)
  Pallas kernels  81.5 us (34%)
  starting transfers between devices  19.8 us (8%)
    all_to_all x3, waiting for transfers between devices, exchange(): return lax.all_to_all(send, both, split_axis=0, concat_axis=0, tiled=True)  132 us
    pallas_call x2, Pallas kernels, filter_call(): pl.pallas_call(functools.partial(filter_kernel, first_slot, groups, per_p...  57.5 us
    all_to_all x3, starting transfers between devices, exchange(): return lax.all_to_all(send, both, split_axis=0, concat_axis=0, tiled=True)  14.5 us
    pallas_call x1, Pallas kernels, body(): pl.pallas_call(functools.partial(galerkin_kernel, chunks, groups, per_pai...  12.7 us
    pallas_call x1, Pallas kernels, body(): pl.pallas_call(functools.partial(applied_kernel, chunks, groups, per_pair...  8.79 us
  transfers between devices with their start and end apart: 8, of which 6 were waited for; matrix products, arithmetic and copies ran while one was open for 1% of the time, Pallas kernels for 29%

profile of v4, /device:TPU:0, one launch (start us, length us, event | category | flops | bytes accessed | tf_op | source)
XLA Modules:
  0.0 240.8 jit_solution(7110565331329737830)
XLA Ops:
  0.6 3.1 %collective-permute-start = (f32[4,64,96]{2,1,0:T(8,128)}, f32[4,64,96]{2,1,0:T(8,128)S(1)}, u32[]{:S(2)}, u32[]{:S(2)}) collective-permute-start(f32[4,64,96]{2,1,0:T(8,128)} %bitcast.7), channel_id=1, source_target_pairs={{0,2},{1,3},{2,0},{3,1},{4,6},{5,7},{6,4},{7,5},{8,10},{9,11},{10,... | collective-permute-start | bytes 294920 | tf_op jit(solution)/shard_map/ppermute | solution.py:237
  3.7 0.8 copy.16.refs_0_
  4.4 0.7 copy-done
  5.1 21.5 %filter0.1 = f32[32,136,128]{2,1,0:T(8,128)} custom-call(s32[16,8]{1,0:T(8,128)S(1)} %copy.16.refs_0_, s32[16]{0:T(128)S(1)} %copy-done, bf16[16,24,4096]{2,1,0:T(8,128)(2,1)} %refs_2_.3, f32[16,4096]{1,0:T(8,128)} %refs_3_.3), custom_call_target="tpu_custom_call" | custom-call | tf_op jit(solution)/shard_map/filter0/pallas_call | solution.py:186
  26.7 4.9 %all-to-all-start = ((f32[32,136,128]{2,1,0:T(8,128)}), f32[32,136,128]{2,1,0:T(8,128)S(1)}, u32[]{:S(2)}, u32[]{:S(2)}) async-start(f32[32,136,128]{2,1,0:T(8,128)} %filter0.1), calls=%async_computation | async-start | bytes 4456448 | tf_op jit(solution)/shard_map/all_to_all | solution.py:431
  31.6 0.3 collective-permute-start.1
  31.9 1.3 collective-permute-done.1
  33.2 36.1 %filter8.1 = f32[32,304,128]{2,1,0:T(8,128)} custom-call(s32[16,8]{1,0:T(8,128)S(1)} %copy.16.refs_0_, s32[16]{0:T(128)S(1)} %copy-done.1, bf16[16,24,4096]{2,1,0:T(8,128)(2,1)} %refs_2_.3, f32[16,4096]{1,0:T(8,128)} %refs_3_.3, f32[16,64,96]{2,1,0:T(8,128)S(1)} %pad_maximum_fusion.refs_4_), custom_call_target="tpu_custom_call" | custom-call | tf_op jit(solution)/shard_map/filter8/pallas_call | solution.py:186
  69.3 13.8 %all-to-all-done.refs_0_ = f32[32,136,128]{2,1,0:T(8,128)S(1)} async-done(((f32[32,136,128]{2,1,0:T(8,128)}), f32[32,136,128]{2,1,0:T(8,128)S(1)}, u32[]{:S(2)}, u32[]{:S(2)}) %all-to-all-start) | async-done | bytes 2228256 | tf_op jit(solution)/shard_map/all_to_all | solution.py:431
  83.1 4.3 %all-to-all-start.1 = ((f32[32,304,128]{2,1,0:T(8,128)}), f32[32,304,128]{2,1,0:T(8,128)}, u32[]{:S(2)}, u32[]{:S(2)}) async-start(f32[32,304,128]{2,1,0:T(8,128)} %filter8.1), calls=%async_computation.1 | async-start | bytes 9961472 | tf_op jit(solution)/shard_map/all_to_all | solution.py:431
  87.6 0.2 div.28.cap_ref
  87.9 0.1 select_reduce_fusion.from_ref
  88.0 110.6 %all-to-all-done.1.refs_1_ = f32[32,304,128]{2,1,0:T(8,128)} async-done(((f32[32,304,128]{2,1,0:T(8,128)}), f32[32,304,128]{2,1,0:T(8,128)}, u32[]{:S(2)}, u32[]{:S(2)}) %all-to-all-start.1) | async-done | bytes 4980768 | tf_op jit(solution)/shard_map/all_to_all | solution.py:431
  198.6 8.8 %applied.1 = f32[32,48,128]{2,1,0:T(8,128)} custom-call(s32[32]{0:T(128)S(1)} %select_reduce_fusion.from_ref, s32[32]{0:T(128)S(1)} %convert_element_type.15.key_ref, f32[4,512]{1,0:T(4,128)S(1)} %div.28.cap_ref, f32[32,136,128]{2,1,0:T(8,128)S(1)} %all-to-all-done.refs_0_, f32[32,304,128]{2,1,0:T(8,128)} %all-to-all-done.1.refs_1_), custom_call_target="tpu_custom_call" | custom-call | tf_op jit(solution)/shard_map/applied/pallas_call | solution.py:458
  207.4 5.3 %all-to-all-start.2 = ((f32[32,48,128]{2,1,0:T(8,128)}), f32[32,48,128]{2,1,0:T(8,128)S(1)}, u32[]{:S(2)}, u32[]{:S(2)}) async-start(f32[32,48,128]{2,1,0:T(8,128)} %applied.1), calls=%async_computation.2 | async-start | bytes 1572864 | tf_op jit(solution)/shard_map/all_to_all | solution.py:431
  212.9 0.2 convert_reduce_fusion
  213.1 12.7 %galerkin.1.after_ref = f32[4,768,768]{2,1,0:T(8,128)} custom-call(s32[32]{0:T(128)S(1)} %select_reduce_fusion.from_ref, f32[4,512]{1,0:T(4,128)S(1)} %div.28.cap_ref, f32[32,136,128]{2,1,0:T(8,128)S(1)} %all-to-all-done.refs_0_, f32[32,304,128]{2,1,0:T(8,128)} %all-to-all-done.1.refs_1_), custom_call_target="tpu_custom_call" | custom-call | tf_op jit(solution)/shard_map/galerkin/pallas_call | solution.py:472
  225.8 7.5 %all-to-all-done.2.in_ref = f32[32,48,128]{2,1,0:T(8,128)S(1)} async-done(((f32[32,48,128]{2,1,0:T(8,128)}), f32[32,48,128]{2,1,0:T(8,128)S(1)}, u32[]{:S(2)}, u32[]{:S(2)}) %all-to-all-start.2) | async-done | bytes 786464 | tf_op jit(solution)/shard_map/all_to_all | solution.py:431
  233.3 1.6 sum_octants.1
  234.9 1.7 collective-permute-start.3
  236.6 0.2 collective-permute-start.4
  236.8 2.0 collective-permute-done.3.refs_2_
  238.8 1.1 collective-permute-done.4.refs_3_
  239.9 0.9 coarse_out.1
  (23 shorter events, 0.6 us)
Async XLA Ops:
  0.6 26.0 %collective-permute-start = (f32[4,64,96]{2,1,0:T(8,128)}, f32[4,64,96]{2,1,0:T(8,128)S(1)}, u32[]{:S(2)}, u32[]{:S(2)}) collective-permute-start(f32[4,64,96]{2,1,0:T(8,128)} %bitcast.7), channel_id=1, source_target_pairs={{0,2},{1,3},{2,0},{3,1},{4,6},{5,7},{6,4},{7,5},{8,10},{9,11},{10,... | collective-permute-start | bytes 294920 | tf_op jit(solution)/shard_map/ppermute | solution.py:237
  4.4 0.7 copy-start
  5.1 21.5 %copy-start.2 = (f32[4,96,64]{1,2,0:T(8,128)S(1)}, f32[4,96,64]{1,2,0:T(8,128)}, u32[]{:S(2)}) copy-start(f32[4,96,64]{1,2,0:T(8,128)} %param.11) | copy-start | bytes 294916
  26.6 6.6 %copy-start.1 = (s32[16]{0:T(128)S(1)}, s32[16]{0:T(128)}, u32[]{:S(2)}) copy-start(s32[16]{0:T(128)} %refs_1_.3) | copy-start | bytes 196
  26.7 56.4 %all-to-all-start = ((f32[32,136,128]{2,1,0:T(8,128)}), f32[32,136,128]{2,1,0:T(8,128)S(1)}, u32[]{:S(2)}, u32[]{:S(2)}) async-start(f32[32,136,128]{2,1,0:T(8,128)} %filter0.1), calls=%async_computation | async-start | bytes 4456448 | tf_op jit(solution)/shard_map/all_to_all | solution.py:431
  31.6 1.6 collective-permute-start.1
  69.3 18.1 %copy-start.4 = (f32[4,512]{1,0:T(4,128)S(1)}, f32[4,512]{1,0:T(4,128)}, u32[]{:S(2)}) copy-start(f32[4,512]{1,0:T(4,128)} %param.10) | copy-start | bytes 24580
  83.1 115.5 %all-to-all-start.1 = ((f32[32,304,128]{2,1,0:T(8,128)}), f32[32,304,128]{2,1,0:T(8,128)}, u32[]{:S(2)}, u32[]{:S(2)}) async-start(f32[32,304,128]{2,1,0:T(8,128)} %filter8.1), calls=%async_computation.1 | async-start | bytes 9961472 | tf_op jit(solution)/shard_map/all_to_all | solution.py:431
  88.0 124.7 %copy-start.3 = (s32[16,8]{0,1:T(8,128)S(1)}, s32[16,8]{0,1:T(8,128)}, u32[]{:S(2)}) copy-start(s32[16,8]{0,1:T(8,128)} %param.9) | copy-start | bytes 1540
  207.4 25.9 %all-to-all-start.2 = ((f32[32,48,128]{2,1,0:T(8,128)}), f32[32,48,128]{2,1,0:T(8,128)S(1)}, u32[]{:S(2)}, u32[]{:S(2)}) async-start(f32[32,48,128]{2,1,0:T(8,128)} %applied.1), calls=%async_computation.2 | async-start | bytes 1572864 | tf_op jit(solution)/shard_map/all_to_all | solution.py:431
  234.9 1.9 collective-permute-start.2
  234.9 3.9 %collective-permute-start.3 = (f32[48,128]{1,0:T(8,128)S(1)}, f32[48,128]{1,0:T(8,128)S(1)}, u32[]{:S(2)}, u32[]{:S(2)}) collective-permute-start(f32[48,128]{1,0:T(8,128)S(1)} %get-tuple-element.16), channel_id=1, source_target_pairs={{0,2},{1,3},{2,0},{3,1},{4,6},{5,7},{6,4},{7,5},{8,10},{9,11},{10,... | collective-permute-start | bytes 73736 | tf_op jit(solution)/shard_map/ppermute | solution.py:499
  236.6 3.3 %collective-permute-start.4 = (f32[48,128]{1,0:T(8,128)S(1)}, f32[48,128]{1,0:T(8,128)S(1)}, u32[]{:S(2)}, u32[]{:S(2)}) collective-permute-start(f32[48,128]{1,0:T(8,128)S(1)} %get-tuple-element.17), channel_id=1, source_target_pairs={{0,3},{1,2},{2,1},{3,0},{4,7},{5,6},{6,5},{7,4},{8,11},{9,10},{10,... | collective-permute-start | bytes 73736 | tf_op jit(solution)/shard_map/ppermute | solution.py:499
